TPU v7x, 512 devices: a whole 4x4x16 slice. The times are simulated.
512 devices in a mesh: section: 8 (over y, z_hi), dp: 16 (over z_lo, core), chan: 4 (over x).
Axes of the slice: x: 4, y: 4, z: 16 (z_hi: 2, z_lo: 8; z = z_hi * 8 + z_lo), core: 2. Of those that a mesh axis runs over, the one named last changes fastest.
Arguments:
- clips: bfloat16 [2, 512, 2048], P(None, 'chan', 'dp'), may hold values from -6 to 6
- weights: bfloat16 [8, 512, 27, 512], P('section', ('chan', 'dp')), may hold values from -0.0546875 to 0.0546875
- cotangents: bfloat16 [2, 512, 2048], P(None, 'chan', 'dp'), may hold values from -0.5 to 0.5
Outputs:
- weight_grads: float32 [8, 512, 27, 512], P('section', ('chan', 'dp'))
All inputs are finite; a program needn't handle non-finite values.
Results may differ from a plain program's by a relative error of at most 0.019.
Values may be sent and summed in bfloat16 or wider, within the bound.
No kernel may reach another device: no remote copies, remote signals or barrier semaphores. Data moves between devices by JAX's collectives and lax.ppermute only.
A program may use at most 128 MiB of HBM per device.

v0:
```python
import jax
import jax.numpy as jnp
from jax import lax
from jax.sharding import PartitionSpec as P

FRAMES = 4
HEIGHT = 4
WIDTH = 8
MICRO = 2


def from_partner(block, axis, distance):
    count = lax.axis_size(axis)
    route = []
    for low in range(count):
        high = low | 1 << distance
        if high != low and high < count:
            route += [(low, high), (high, low)]
    return lax.ppermute(block, axis, route)


def with_halo(shard, sides, width):
    for axis, dim in sides:
        size, length = (lax.axis_size(axis), shard.shape[dim])
        up = [(i, (i + 1) % size) for i in range(size - 1)]
        down = [(j, i) for i, j in up]
        last = lax.slice_in_dim(shard, length - width, length, axis=dim)
        first = lax.slice_in_dim(shard, 0, width, axis=dim)
        before = lax.ppermute(last, axis, up)
        after = lax.ppermute(first, axis, down)
        shard = jnp.concatenate([before, shard, after], axis=dim)
    return shard


def as_sent(shard):

    def short(part):
        return part.astype(jnp.bfloat16) if part.dtype == jnp.float32 else part

    return jax.tree.map(short, shard)


def silu_slope(values):
    sigmoid = jax.nn.sigmoid(values)
    return sigmoid * (1.0 + values * (1.0 - sigmoid))


def shifted_taps(source, time_shift, mirror, frames, height, columns):
    cell_count = source.shape[1]
    plane_size = height * columns
    margin = plane_size + columns + 1
    padded = jnp.pad(source, ((0, 0), (margin, margin)))
    position = jnp.arange(cell_count, dtype=jnp.int32)
    frame_of = position // plane_size % frames
    row_of = position // columns % height
    column_of = position % columns
    windows = []
    for row_shift in range(3):
        for column_shift in range(3):
            if mirror:
                move_frame, move_row, move_column = (
                    1 - time_shift,
                    1 - row_shift,
                    1 - column_shift,
                )
            else:
                move_frame, move_row, move_column = (
                    time_shift - 1,
                    row_shift - 1,
                    column_shift - 1,
                )
            offset = move_frame * plane_size + move_row * columns + move_column
            window = padded[:, margin + offset : margin + offset + cell_count]
            inside = (
                (frame_of + move_frame >= 0)
                & (frame_of + move_frame < frames)
                & (row_of + move_row >= 0)
                & (row_of + move_row < height)
                & (column_of + move_column >= 0)
                & (column_of + move_column < columns)
            )
            windows.append(jnp.where(inside[None, :], window, jnp.zeros_like(window)))
    return windows


def arrange_kernel(kernel):
    outputs = kernel.shape[0]
    inputs = kernel.shape[2]
    return kernel.reshape(outputs, 3, 9 * inputs).transpose(1, 0, 2)


def conv_forward(activated, arranged, frames, height, columns):
    outputs = arranged.shape[1]
    result = jnp.zeros((outputs, activated.shape[1]), jnp.float32)
    for time_shift in range(3):
        stacked = jnp.concatenate(
            shifted_taps(activated, time_shift, False, frames, height, columns), axis=0
        )
        result = result + jnp.dot(arranged[time_shift], stacked, preferred_element_type=jnp.float32)
    return result


def conv_input_grad(grads_all, arranged, frames, height, columns):
    outputs = arranged.shape[1]
    inputs = arranged.shape[2] // 9
    cell_count = grads_all.shape[1]
    result = jnp.zeros((inputs, cell_count), jnp.float32)
    for time_shift in range(3):
        stacked = jnp.stack(
            shifted_taps(grads_all, time_shift, True, frames, height, columns), axis=1
        )
        stacked = stacked.reshape(-1, cell_count)
        matrix = arranged[time_shift].reshape(outputs * 9, inputs)
        result = result + lax.dot_general(
            matrix, stacked, (((0,), (0,)), ((), ())), preferred_element_type=jnp.float32
        )
    return result


def weight_grad_from_grads(activated, grad_low, frames, height, columns):
    outputs = grad_low.shape[0]
    cell_count = grad_low.shape[1]
    pieces = []
    for time_shift in range(3):
        stacked = jnp.stack(
            shifted_taps(grad_low, time_shift, True, frames, height, columns), axis=1
        )
        stacked = stacked.reshape(outputs * 9, cell_count)
        product = lax.dot_general(
            stacked, activated, (((1,), (1,)), ((), ())), preferred_element_type=jnp.float32
        )
        pieces.append(product.reshape(outputs, 9, activated.shape[0]))
    return jnp.concatenate(pieces, axis=1)


def mirror_pair(source):
    for bit_index in range(lax.axis_size("section").bit_length() - 1):
        source = from_partner(source, "section", bit_index)
    return source


def kernel_mirror(source):
    for bit_index in range(lax.axis_size("section").bit_length() - 1):
        source = from_partner(source, "section", bit_index)
    return source


def mirror_grads(source):
    for bit_index in range(lax.axis_size("section").bit_length() - 1):
        source = from_partner(source.astype(jnp.bfloat16), "section", bit_index).astype(
            source.dtype
        )
    return source


def channel_gather(source):
    return lax.all_gather(source, "chan", axis=0, tiled=True)


def section_rims(source):
    return with_halo(source[None], (("section", 0),), 1)


def active_lane(tick_index, positions, spacing, per_lane, lane_count):
    offsets = tick_index - positions
    first_aligned = offsets[0] % spacing == 0
    lane_now = jnp.where(first_aligned, 0, lane_count - 1).astype(jnp.int32)
    offset = jnp.where(first_aligned, offsets[0], offsets[lane_count - 1])
    slot_now = offset // spacing
    is_valid = (offset % spacing == 0) & (slot_now >= 0) & (slot_now < per_lane)
    return (lane_now, jnp.clip(slot_now, 0, per_lane - 1), is_valid)


def store_slot(buffer, lane_now, slot_now, is_valid, payload):
    chosen = jnp.where(is_valid, payload, buffer[lane_now, slot_now])
    starts = (lane_now, slot_now) + (0,) * payload.ndim
    return lax.dynamic_update_slice(buffer, chosen[None, None], starts)


def receive_slots(buffer, anchors, keep_mask, tick_index, spacing, per_lane, payload):
    for lane_index in range(anchors.shape[0]):
        offset = tick_index - anchors[lane_index]
        slot_now = offset // spacing
        is_valid = (
            keep_mask[lane_index]
            & (offset % spacing == 0)
            & (slot_now >= 0)
            & (slot_now < per_lane)
        )
        buffer = store_slot(
            buffer, lane_index, jnp.clip(slot_now, 0, per_lane - 1), is_valid, payload
        )
    return buffer


def branch_index(is_valid, lane_now):
    return jnp.where(is_valid, lane_now + 1, 0)


def on_device(clips, weights, cotangents):
    sections = lax.axis_size("section")
    section_id = lax.axis_index("section")
    half_depth = sections // 2
    local_rows = clips.shape[1]
    cell_count = clips.shape[2]
    channels = local_rows * lax.axis_size("chan")
    own_share = weights[0]
    lane_shares = jnp.stack([own_share, kernel_mirror(own_share)])
    lane_layers = jnp.stack([section_id, sections - 1 - section_id])
    lane_first = jnp.array([0, MICRO // 2], jnp.int32)
    per_lane = MICRO // 2
    spacing = 2
    lane_count = lane_shares.shape[0]
    lane_kernels = lax.all_gather(lane_shares, "dp", axis=1, tiled=True)
    arranged_lanes = [arrange_kernel(lane_kernels[lane_index]) for lane_index in range(lane_count)]
    tick_count = sections + spacing * (per_lane - 1)

    def forward_tick(tick_index, carried):
        incoming, inputs_buf, skip_buf, acts_buf = carried
        lane_now, slot_now, is_valid = active_lane(
            tick_index, lane_layers, spacing, per_lane, lane_count
        )
        layer_now = lane_layers[lane_now]
        clip_now = clips[lane_first[lane_now] + slot_now]
        state_now = jnp.where(layer_now == 0, clip_now, incoming[lane_now])
        skip_now = skip_buf[lane_now, slot_now]
        summed = state_now.astype(jnp.float32) + skip_now.astype(jnp.float32)
        activated = jax.nn.silu(summed).astype(jnp.bfloat16)
        acts_all = channel_gather(activated)

        def forward_skipped():
            return jnp.zeros(state_now.shape, jnp.float32)

        def forward_make_branch(lane_index):

            def convolve():
                return conv_forward(acts_all, arranged_lanes[lane_index], FRAMES, HEIGHT, WIDTH)

            return convolve

        branches = [forward_skipped] + [
            forward_make_branch(lane_index) for lane_index in range(lane_count)
        ]
        update = lax.switch(branch_index(is_valid, lane_now), branches)
        output = (state_now.astype(jnp.float32) + update).astype(jnp.bfloat16)
        inputs_buf = store_slot(inputs_buf, lane_now, slot_now, is_valid, state_now)
        acts_buf = store_slot(acts_buf, lane_now, slot_now, is_valid, acts_all)
        outgoing = jnp.where(is_valid & (layer_now < half_depth), output, jnp.zeros_like(output))
        arrived = mirror_pair(outgoing)
        skip_buf = receive_slots(
            skip_buf,
            sections - 1 - lane_layers,
            lane_layers >= half_depth,
            tick_index,
            spacing,
            per_lane,
            arrived,
        )
        rim_rows = section_rims(output)
        incoming = jnp.stack([rim_rows[0], rim_rows[2]])
        return (incoming, inputs_buf, skip_buf, acts_buf)

    empty_rows = jnp.zeros((lane_count, local_rows, cell_count), jnp.bfloat16)
    empty_slots = jnp.zeros((lane_count, per_lane, local_rows, cell_count), jnp.bfloat16)
    empty_acts = jnp.zeros((lane_count, per_lane, channels, cell_count), jnp.bfloat16)
    forward_out = lax.fori_loop(
        0, tick_count, forward_tick, (empty_rows, empty_slots, empty_slots, empty_acts)
    )
    inputs_buf, skip_buf, acts_buf = (forward_out[1], forward_out[2], forward_out[3])

    def backward_tick(tick_index, carried):
        incoming, gskip_buf, glow_buf = carried
        lane_now, slot_now, is_valid = active_lane(
            tick_index, sections - 1 - lane_layers, spacing, per_lane, lane_count
        )
        layer_now = lane_layers[lane_now]
        cotangent_now = cotangents[lane_first[lane_now] + slot_now]
        upstream = jnp.where(layer_now == sections - 1, cotangent_now, incoming[lane_now]).astype(
            jnp.float32
        )
        upstream = upstream + gskip_buf[lane_now, slot_now].astype(jnp.float32)
        grad_low = upstream.astype(jnp.bfloat16)
        summed = inputs_buf[lane_now, slot_now].astype(jnp.float32) + skip_buf[
            lane_now, slot_now
        ].astype(jnp.float32)

        def backward_skipped():
            return jnp.zeros((channels, cell_count), jnp.float32)

        def backward_make_branch(lane_index):

            def differentiate():
                return conv_input_grad(grad_low, arranged_lanes[lane_index], FRAMES, HEIGHT, WIDTH)

            return differentiate

        branches = [backward_skipped] + [
            backward_make_branch(lane_index) for lane_index in range(lane_count)
        ]
        partial_terms = lax.switch(branch_index(is_valid, lane_now), branches)
        pre_grad = jax.tree.map(
            lambda part: part.astype(jnp.float32),
            lax.psum_scatter(as_sent(partial_terms), "chan", scatter_dimension=0, tiled=True),
        ) * silu_slope(summed)
        glow_buf = store_slot(glow_buf, lane_now, slot_now, is_valid, grad_low)
        sent = (upstream + pre_grad).astype(jnp.bfloat16)
        skip_low = pre_grad.astype(jnp.bfloat16)
        outgoing = jnp.where(
            is_valid & (layer_now >= half_depth), skip_low, jnp.zeros_like(skip_low)
        )
        arrived = mirror_pair(outgoing)
        gskip_buf = receive_slots(
            gskip_buf, lane_layers, lane_layers < half_depth, tick_index, spacing, per_lane, arrived
        )
        rim_rows = section_rims(sent)
        incoming = jnp.stack([rim_rows[2], rim_rows[0]])
        return (incoming, gskip_buf, glow_buf)

    backward_out = lax.fori_loop(
        0, tick_count, backward_tick, (empty_rows, empty_slots, empty_slots)
    )
    glow_buf = backward_out[2]
    grads_rows = lax.all_to_all(glow_buf, "dp", split_axis=2, concat_axis=3, tiled=True)
    acts_cells = lax.all_gather(acts_buf, "dp", axis=3, tiled=True)
    lane_grads = []
    for lane_index in range(lane_count):
        total = weight_grad_from_grads(
            acts_cells[lane_index, 0], grads_rows[lane_index, 0], FRAMES, HEIGHT, WIDTH
        )
        lane_grads.append(total)
    own_grads = lane_grads[0] + mirror_grads(lane_grads[1])
    return own_grads[None]


def solution(mesh):
    placed = (
        P(None, "chan", "dp"),
        P("section", ("chan", "dp"), None, None),
        P(None, "chan", "dp"),
    )
    return jax.shard_map(
        on_device,
        mesh=mesh,
        in_specs=placed,
        out_specs=P("section", ("chan", "dp"), None, None),
        check_vma=False,
    )
```

profile of v0, /device:TPU:8, one launch (start us, length us, event | category | flops | bytes accessed | tf_op | source)
XLA Modules:
  0.0 1673.4 jit_solution(5137266346502927320)
XLA Ops:
  6.5 15.7 collective-permute-start.10
  62.8 129.0 %all-gather.3.cloned.1.call-done = bf16[2,128,27,512]{3,0,2,1:T(2,128)(2,1)} async-done(((bf16[2,8,27,512]{3,0,2,1:T(2,128)(2,1)}), bf16[2,128,27,512]{3,0,2,1:T(2,128)(2,1)}) %all-gather.3.cloned.1.call-update) | async-done | bytes 7077904 | tf_op jit(solution)/shard_map/all_gather | solution.py:214
  191.8 15.5 fusion.311
  207.2 14.8 copy.1660
  226.2 14.8 copy.1661
  245.3 529.0 %while.42 = (s32[]{:T(128)}, bf16[2,128,128]{1,2,0:T(8,128)(2,1)S(1)}, bf16[2,1,128,128]{2,3,1,0:T(8,128)(2,1)S(1)}, bf16[2,1,128,128]{2,3,1,0:T(8,128)(2,1)S(1)...) while((s32[]{:T(128)}, ...), condition=%wide.region_4.5_spmd, body=%wide.region_0.4_spmd.sunk | while | flops 455368896 | bytes 31049684 | solution.py:266
  253.3 11.5 all_gather.20
  264.8 7.4 collective-permute-start
  280.1 8.2 collective-permute-start.2
  294.6 7.7 collective-permute-start.3
  321.0 10.7 all_gather.20
  331.7 9.2 collective-permute-start
  350.9 10.5 collective-permute-done.2
  384.3 10.8 all_gather.20
  403.4 11.6 collective-permute-start.1
  419.8 10.5 collective-permute-done.2
  451.3 10.7 all_gather.20
  467.7 8.9 collective-permute-start.1
  477.3 11.3 collective-permute-start.2
  515.1 10.8 all_gather.20
  525.9 10.2 collective-permute-start
  543.1 13.5 collective-permute-start.2
  564.3 8.3 collective-permute-start.4
  582.4 10.7 all_gather.20
  603.9 9.1 collective-permute-start.1
  619.2 9.0 collective-permute-done.2
  649.3 11.1 all_gather.20
  660.4 13.2 collective-permute-start
  676.3 7.7 collective-permute-start.2
  713.3 10.7 all_gather.20
  724.0 12.4 collective-permute-start
  739.3 13.3 collective-permute-start.2
  754.5 9.0 collective-permute-start.3
  775.6 744.8 %while.43 = (s32[]{:T(128)}, bf16[2,128,128]{1,2,0:T(8,128)(2,1)S(1)}, bf16[2,1,128,128]{2,3,1,0:T(8,128)(2,1)}, bf16[2,1,128,128]{2,3,1,0:T(8,128)(2,1)}, s32[2...) while((s32[]{:T(128)}, ...), condition=%wide.region_10.11_spmd, body=%wide.region_5.10_spmd.sunk | while | flops 454528576 | bytes 34589428 | solution.py:319
  787.0 36.6 %reduce-scatter.6.cloned.1.call-done = bf16[128,128]{1,0:T(8,128)(2,1)} async-done(((bf16[512,128]{1,0:T(8,128)(2,1)}), bf16[128,128]{1,0:T(8,128)(2,1)}) %reduce-scatter.6.cloned.1.call-update) | async-done | bytes 32784 | tf_op jit(solution)/shard_map/while
  825.3 12.8 collective-permute-start.7
  840.9 13.5 collective-permute-start.6
  881.8 35.2 %reduce-scatter.6.cloned.1.call-done = bf16[128,128]{1,0:T(8,128)(2,1)} async-done(((bf16[512,128]{1,0:T(8,128)(2,1)}), bf16[128,128]{1,0:T(8,128)(2,1)}) %reduce-scatter.6.cloned.1.call-update) | async-done | bytes 32784 | tf_op jit(solution)/shard_map/while
  918.6 12.8 collective-permute-start.7
  934.2 13.5 collective-permute-start.6
  973.5 17.4 %conditional.5 = (bf16[512,128]{0,1:T(8,128)(2,1)S(1)}) conditional(s32[]{:T(128)} %clamp.25, () %tuple.419, (bf16[128,128]{0,1:T(8,128)(2,1)S(1)}, bf16[3,128,4608]{2,1,0:T(8,128)(2,1)}) %tuple.420, (bf16[128,128]{0,1:T(8,128)(2,1)S(1)}, bf16[3,128,4608]{2,1,0:T(8,128)(2,1)}) %tuple.421), branch_computations={%region_6.6_spmd, %region_7.7_spmd, %region_8.8_spmd} | conditional | flops 453791232 | bytes 30786196 | solution.py:300
  992.4 17.1 %reduce-scatter.6.cloned.1.call-done = bf16[128,128]{1,0:T(8,128)(2,1)} async-done(((bf16[512,128]{1,0:T(8,128)(2,1)}), bf16[128,128]{1,0:T(8,128)(2,1)}) %reduce-scatter.6.cloned.1.call-update) | async-done | bytes 32784 | tf_op jit(solution)/shard_map/while
  1011.2 12.8 collective-permute-start.7
  1026.8 13.5 collective-permute-start.6
  1067.6 35.2 %reduce-scatter.6.cloned.1.call-done = bf16[128,128]{1,0:T(8,128)(2,1)} async-done(((bf16[512,128]{1,0:T(8,128)(2,1)}), bf16[128,128]{1,0:T(8,128)(2,1)}) %reduce-scatter.6.cloned.1.call-update) | async-done | bytes 32784 | tf_op jit(solution)/shard_map/while
  1104.6 12.8 collective-permute-start.7
  1120.2 13.5 collective-permute-start.6
  1161.0 35.2 %reduce-scatter.6.cloned.1.call-done = bf16[128,128]{1,0:T(8,128)(2,1)} async-done(((bf16[512,128]{1,0:T(8,128)(2,1)}), bf16[128,128]{1,0:T(8,128)(2,1)}) %reduce-scatter.6.cloned.1.call-update) | async-done | bytes 32784 | tf_op jit(solution)/shard_map/while
  1197.9 12.8 collective-permute-start.7
  1213.5 13.5 collective-permute-start.6
  1252.8 17.4 %conditional.5 = (bf16[512,128]{0,1:T(8,128)(2,1)S(1)}) conditional(s32[]{:T(128)} %clamp.25, () %tuple.419, (bf16[128,128]{0,1:T(8,128)(2,1)S(1)}, bf16[3,128,4608]{2,1,0:T(8,128)(2,1)}) %tuple.420, (bf16[128,128]{0,1:T(8,128)(2,1)S(1)}, bf16[3,128,4608]{2,1,0:T(8,128)(2,1)}) %tuple.421), branch_computations={%region_6.6_spmd, %region_7.7_spmd, %region_8.8_spmd} | conditional | flops 453791232 | bytes 30786196 | solution.py:300
  1271.7 17.0 %reduce-scatter.6.cloned.1.call-done = bf16[128,128]{1,0:T(8,128)(2,1)} async-done(((bf16[512,128]{1,0:T(8,128)(2,1)}), bf16[128,128]{1,0:T(8,128)(2,1)}) %reduce-scatter.6.cloned.1.call-update) | async-done | bytes 32784 | tf_op jit(solution)/shard_map/while
  1290.5 12.8 collective-permute-start.7
  1306.1 13.5 collective-permute-start.6
  1346.9 35.2 %reduce-scatter.6.cloned.1.call-done = bf16[128,128]{1,0:T(8,128)(2,1)} async-done(((bf16[512,128]{1,0:T(8,128)(2,1)}), bf16[128,128]{1,0:T(8,128)(2,1)}) %reduce-scatter.6.cloned.1.call-update) | async-done | bytes 32784 | tf_op jit(solution)/shard_map/while
  1383.7 12.8 collective-permute-start.7
  1399.4 13.5 collective-permute-start.6
  1440.2 33.5 %reduce-scatter.6.cloned.1.call-done = bf16[128,128]{1,0:T(8,128)(2,1)} async-done(((bf16[512,128]{1,0:T(8,128)(2,1)}), bf16[128,128]{1,0:T(8,128)(2,1)}) %reduce-scatter.6.cloned.1.call-update) | async-done | bytes 32784 | tf_op jit(solution)/shard_map/while
  1475.4 12.8 collective-permute-start.7
  1491.0 13.5 collective-permute-start.6
  1526.6 10.6 all-to-all-done
  1557.2 66.0 %all-gather.5.cloned.1.call-done = bf16[2,1,512,2048]{2,3,1,0:T(8,128)(2,1)} async-done(((bf16[2,1,512,128]{2,3,1,0:T(8,128)(2,1)}), bf16[2,1,512,2048]{2,3,1,0:T(8,128)(2,1)}) %all-gather.5.cloned.1.call-update) | async-done | bytes 4194320 | tf_op jit(solution)/shard_map/all_gather | solution.py:324
  1628.0 7.6 collective-permute-start.13
  1636.1 10.5 collective-permute-done.13
  (906 shorter events, 526.8 us)
Async XLA Ops:
  6.5 185.2 %all-gather.3.cloned.1.call-start = ((), (), s32[]{:S(2)}) async-start(), calls=%async_computation.2 | async-start | bytes 7520256 | tf_op jit(solution)/shard_map/all_gather | solution.py:214
  6.5 21.6 %collective-permute-start.10 = (bf16[8,27,512]{2,0,1:T(8,128)(2,1)}, bf16[8,27,512]{2,0,1:T(8,128)(2,1)S(1)}, u32[]{:S(2)}, u32[]{:S(2)}) collective-permute-start(bf16[8,27,512]{2,0,1:T(8,128)(2,1)} %bitcast.642), channel_id=1, source_target_pairs={{0,64},{64,0},{128,192},{192,128},{256,320},{320,256},{384,448},{4... | collective-permute-start | bytes 663560 | tf_op jit(solution)/shard_map/ppermute | solution.py:19
  264.8 42.8 %collective-permute-start = (bf16[1,128,128]{1,2,0:T(8,128)(2,1)S(1)}, bf16[1,128,128]{1,2,0:T(8,128)(2,1)S(1)}, u32[]{:S(2)}, u32[]{:S(2)}) collective-permute-start(bf16[1,128,128]{1,2,0:T(8,128)(2,1)S(1)} %fusion.351), channel_id=1, source_target_pairs={{64,0},{128,64},{192,128},{256,192},{320,256},{384,320},{448,384},... | collective-permute-start | bytes 98312 | tf_op jit(solution)/shard_map/while/body/eval_jaxpr/ppermute | solution.py:30
  272.2 35.5 %collective-permute-start.1 = (bf16[1,128,128]{1,2,0:T(8,128)(2,1)S(1)}, bf16[1,128,128]{1,2,0:T(8,128)(2,1)S(1)}, u32[]{:S(2)}, u32[]{:S(2)}) collective-permute-start(bf16[1,128,128]{1,2,0:T(8,128)(2,1)S(1)} %fusion.351), channel_id=1, source_target_pairs={{0,64},{64,128},{128,192},{192,256},{256,320},{320,384},{384,448},... | collective-permute-start | bytes 98312 | tf_op jit(solution)/shard_map/while/body/eval_jaxpr/ppermute | solution.py:29
  280.1 14.5 collective-permute-start.2
  294.6 11.1 collective-permute-start.3
  331.7 42.8 %collective-permute-start = (bf16[1,128,128]{1,2,0:T(8,128)(2,1)S(1)}, bf16[1,128,128]{1,2,0:T(8,128)(2,1)S(1)}, u32[]{:S(2)}, u32[]{:S(2)}) collective-permute-start(bf16[1,128,128]{1,2,0:T(8,128)(2,1)S(1)} %fusion.351), channel_id=1, source_target_pairs={{64,0},{128,64},{192,128},{256,192},{320,256},{384,320},{448,384},... | collective-permute-start | bytes 98312 | tf_op jit(solution)/shard_map/while/body/eval_jaxpr/ppermute | solution.py:30
  340.9 33.7 %collective-permute-start.1 = (bf16[1,128,128]{1,2,0:T(8,128)(2,1)S(1)}, bf16[1,128,128]{1,2,0:T(8,128)(2,1)S(1)}, u32[]{:S(2)}, u32[]{:S(2)}) collective-permute-start(bf16[1,128,128]{1,2,0:T(8,128)(2,1)S(1)} %fusion.351), channel_id=1, source_target_pairs={{0,64},{64,128},{128,192},{192,256},{256,320},{320,384},{384,448},... | collective-permute-start | bytes 98312 | tf_op jit(solution)/shard_map/while/body/eval_jaxpr/ppermute | solution.py:29
  347.0 14.5 collective-permute-start.2
  400.5 37.5 %collective-permute-start = (bf16[1,128,128]{1,2,0:T(8,128)(2,1)S(1)}, bf16[1,128,128]{1,2,0:T(8,128)(2,1)S(1)}, u32[]{:S(2)}, u32[]{:S(2)}) collective-permute-start(bf16[1,128,128]{1,2,0:T(8,128)(2,1)S(1)} %fusion.351), channel_id=1, source_target_pairs={{64,0},{128,64},{192,128},{256,192},{320,256},{384,320},{448,384},... | collective-permute-start | bytes 98312 | tf_op jit(solution)/shard_map/while/body/eval_jaxpr/ppermute | solution.py:30
  403.4 34.6 %collective-permute-start.1 = (bf16[1,128,128]{1,2,0:T(8,128)(2,1)S(1)}, bf16[1,128,128]{1,2,0:T(8,128)(2,1)S(1)}, u32[]{:S(2)}, u32[]{:S(2)}) collective-permute-start(bf16[1,128,128]{1,2,0:T(8,128)(2,1)S(1)} %fusion.351), channel_id=1, source_target_pairs={{0,64},{64,128},{128,192},{192,256},{256,320},{320,384},{384,448},... | collective-permute-start | bytes 98312 | tf_op jit(solution)/shard_map/while/body/eval_jaxpr/ppermute | solution.py:29
  415.8 14.5 collective-permute-start.2
  462.0 43.3 %collective-permute-start = (bf16[1,128,128]{1,2,0:T(8,128)(2,1)S(1)}, bf16[1,128,128]{1,2,0:T(8,128)(2,1)S(1)}, u32[]{:S(2)}, u32[]{:S(2)}) collective-permute-start(bf16[1,128,128]{1,2,0:T(8,128)(2,1)S(1)} %fusion.351), channel_id=1, source_target_pairs={{64,0},{128,64},{192,128},{256,192},{320,256},{384,320},{448,384},... | collective-permute-start | bytes 98312 | tf_op jit(solution)/shard_map/while/body/eval_jaxpr/ppermute | solution.py:30
  467.7 37.6 %collective-permute-start.1 = (bf16[1,128,128]{1,2,0:T(8,128)(2,1)S(1)}, bf16[1,128,128]{1,2,0:T(8,128)(2,1)S(1)}, u32[]{:S(2)}, u32[]{:S(2)}) collective-permute-start(bf16[1,128,128]{1,2,0:T(8,128)(2,1)S(1)} %fusion.351), channel_id=1, source_target_pairs={{0,64},{64,128},{128,192},{192,256},{256,320},{320,384},{384,448},... | collective-permute-start | bytes 98312 | tf_op jit(solution)/shard_map/while/body/eval_jaxpr/ppermute | solution.py:29
  477.3 14.5 collective-permute-start.2
  525.9 46.7 %collective-permute-start = (bf16[1,128,128]{1,2,0:T(8,128)(2,1)S(1)}, bf16[1,128,128]{1,2,0:T(8,128)(2,1)S(1)}, u32[]{:S(2)}, u32[]{:S(2)}) collective-permute-start(bf16[1,128,128]{1,2,0:T(8,128)(2,1)S(1)} %fusion.351), channel_id=1, source_target_pairs={{64,0},{128,64},{192,128},{256,192},{320,256},{384,320},{448,384},... | collective-permute-start | bytes 98312 | tf_op jit(solution)/shard_map/while/body/eval_jaxpr/ppermute | solution.py:30
  536.1 36.6 %collective-permute-start.1 = (bf16[1,128,128]{1,2,0:T(8,128)(2,1)S(1)}, bf16[1,128,128]{1,2,0:T(8,128)(2,1)S(1)}, u32[]{:S(2)}, u32[]{:S(2)}) collective-permute-start(bf16[1,128,128]{1,2,0:T(8,128)(2,1)S(1)} %fusion.351), channel_id=1, source_target_pairs={{0,64},{64,128},{128,192},{192,256},{256,320},{320,384},{384,448},... | collective-permute-start | bytes 98312 | tf_op jit(solution)/shard_map/while/body/eval_jaxpr/ppermute | solution.py:29
  543.1 15.4 collective-permute-start.2
  564.3 10.2 collective-permute-start.4
  598.4 37.5 %collective-permute-start = (bf16[1,128,128]{1,2,0:T(8,128)(2,1)S(1)}, bf16[1,128,128]{1,2,0:T(8,128)(2,1)S(1)}, u32[]{:S(2)}, u32[]{:S(2)}) collective-permute-start(bf16[1,128,128]{1,2,0:T(8,128)(2,1)S(1)} %fusion.351), channel_id=1, source_target_pairs={{64,0},{128,64},{192,128},{256,192},{320,256},{384,320},{448,384},... | collective-permute-start | bytes 98312 | tf_op jit(solution)/shard_map/while/body/eval_jaxpr/ppermute | solution.py:30
  603.9 32.0 %collective-permute-start.1 = (bf16[1,128,128]{1,2,0:T(8,128)(2,1)S(1)}, bf16[1,128,128]{1,2,0:T(8,128)(2,1)S(1)}, u32[]{:S(2)}, u32[]{:S(2)}) collective-permute-start(bf16[1,128,128]{1,2,0:T(8,128)(2,1)S(1)} %fusion.351), channel_id=1, source_target_pairs={{0,64},{64,128},{128,192},{192,256},{256,320},{320,384},{384,448},... | collective-permute-start | bytes 98312 | tf_op jit(solution)/shard_map/while/body/eval_jaxpr/ppermute | solution.py:29
  613.7 14.5 collective-permute-start.2
  660.4 43.2 %collective-permute-start = (bf16[1,128,128]{1,2,0:T(8,128)(2,1)S(1)}, bf16[1,128,128]{1,2,0:T(8,128)(2,1)S(1)}, u32[]{:S(2)}, u32[]{:S(2)}) collective-permute-start(bf16[1,128,128]{1,2,0:T(8,128)(2,1)S(1)} %fusion.351), channel_id=1, source_target_pairs={{64,0},{128,64},{192,128},{256,192},{320,256},{384,320},{448,384},... | collective-permute-start | bytes 98312 | tf_op jit(solution)/shard_map/while/body/eval_jaxpr/ppermute | solution.py:30
  673.6 29.9 %collective-permute-start.1 = (bf16[1,128,128]{1,2,0:T(8,128)(2,1)S(1)}, bf16[1,128,128]{1,2,0:T(8,128)(2,1)S(1)}, u32[]{:S(2)}, u32[]{:S(2)}) collective-permute-start(bf16[1,128,128]{1,2,0:T(8,128)(2,1)S(1)} %fusion.351), channel_id=1, source_target_pairs={{0,64},{64,128},{128,192},{192,256},{256,320},{320,384},{384,448},... | collective-permute-start | bytes 98312 | tf_op jit(solution)/shard_map/while/body/eval_jaxpr/ppermute | solution.py:29
  676.3 14.6 collective-permute-start.2
  724.0 44.8 %collective-permute-start = (bf16[1,128,128]{1,2,0:T(8,128)(2,1)S(1)}, bf16[1,128,128]{1,2,0:T(8,128)(2,1)S(1)}, u32[]{:S(2)}, u32[]{:S(2)}) collective-permute-start(bf16[1,128,128]{1,2,0:T(8,128)(2,1)S(1)} %fusion.351), channel_id=1, source_target_pairs={{64,0},{128,64},{192,128},{256,192},{320,256},{384,320},{448,384},... | collective-permute-start | bytes 98312 | tf_op jit(solution)/shard_map/while/body/eval_jaxpr/ppermute | solution.py:30
  736.4 32.4 %collective-permute-start.1 = (bf16[1,128,128]{1,2,0:T(8,128)(2,1)S(1)}, bf16[1,128,128]{1,2,0:T(8,128)(2,1)S(1)}, u32[]{:S(2)}, u32[]{:S(2)}) collective-permute-start(bf16[1,128,128]{1,2,0:T(8,128)(2,1)S(1)} %fusion.351), channel_id=1, source_target_pairs={{0,64},{64,128},{128,192},{192,256},{256,320},{320,384},{384,448},... | collective-permute-start | bytes 98312 | tf_op jit(solution)/shard_map/while/body/eval_jaxpr/ppermute | solution.py:29
  739.3 15.2 collective-permute-start.2
  754.5 12.4 collective-permute-start.3
  775.6 48.0 %reduce-scatter.6.cloned.1.call-start = ((), (), s32[]{:S(2)}) async-start(), calls=%async_computation.4 | async-start | bytes 163840 | tf_op jit(solution)/shard_map/while
  825.3 29.2 %collective-permute-start.7 = (bf16[128,128]{0,1:T(8,128)(2,1)S(1)}, bf16[128,128]{0,1:T(8,128)(2,1)S(1)}, u32[]{:S(2)}, u32[]{:S(2)}) collective-permute-start(bf16[128,128]{0,1:T(8,128)(2,1)S(1)} %convert_select_fusion.2), channel_id=1, source_target_pairs={{0,64},{64,0},{128,192},{192,128},{256,320},{320,256},{384,448},{4... | collective-permute-start | bytes 98312 | tf_op jit(solution)/shard_map/while/body/eval_jaxpr/ppermute | solution.py:19
  839.0 25.5 %collective-permute-start.5 = (bf16[1,128,128]{1,2,0:T(8,128)(2,1)S(1)}, bf16[1,128,128]{1,2,0:T(8,128)(2,1)S(1)}, u32[]{:S(2)}, u32[]{:S(2)}) collective-permute-start(bf16[1,128,128]{1,2,0:T(8,128)(2,1)S(1)} %fusion.357), channel_id=1, source_target_pairs={{0,64},{64,128},{128,192},{192,256},{256,320},{320,384},{384,448},... | collective-permute-start | bytes 98312 | tf_op jit(solution)/shard_map/while/body/eval_jaxpr/ppermute | solution.py:29
  840.9 23.6 %collective-permute-start.6 = (bf16[1,128,128]{1,2,0:T(8,128)(2,1)S(1)}, bf16[1,128,128]{1,2,0:T(8,128)(2,1)S(1)}, u32[]{:S(2)}, u32[]{:S(2)}) collective-permute-start(bf16[1,128,128]{1,2,0:T(8,128)(2,1)S(1)} %fusion.357), channel_id=1, source_target_pairs={{64,0},{128,64},{192,128},{256,192},{320,256},{384,320},{448,384},... | collective-permute-start | bytes 98312 | tf_op jit(solution)/shard_map/while/body/eval_jaxpr/ppermute | solution.py:30
  870.3 46.6 %reduce-scatter.6.cloned.1.call-start = ((), (), s32[]{:S(2)}) async-start(), calls=%async_computation.4 | async-start | bytes 163840 | tf_op jit(solution)/shard_map/while
  918.6 29.2 %collective-permute-start.7 = (bf16[128,128]{0,1:T(8,128)(2,1)S(1)}, bf16[128,128]{0,1:T(8,128)(2,1)S(1)}, u32[]{:S(2)}, u32[]{:S(2)}) collective-permute-start(bf16[128,128]{0,1:T(8,128)(2,1)S(1)} %convert_select_fusion.2), channel_id=1, source_target_pairs={{0,64},{64,0},{128,192},{192,128},{256,320},{320,256},{384,448},{4... | collective-permute-start | bytes 98312 | tf_op jit(solution)/shard_map/while/body/eval_jaxpr/ppermute | solution.py:19
  932.3 25.6 %collective-permute-start.5 = (bf16[1,128,128]{1,2,0:T(8,128)(2,1)S(1)}, bf16[1,128,128]{1,2,0:T(8,128)(2,1)S(1)}, u32[]{:S(2)}, u32[]{:S(2)}) collective-permute-start(bf16[1,128,128]{1,2,0:T(8,128)(2,1)S(1)} %fusion.357), channel_id=1, source_target_pairs={{0,64},{64,128},{128,192},{192,256},{256,320},{320,384},{384,448},... | collective-permute-start | bytes 98312 | tf_op jit(solution)/shard_map/while/body/eval_jaxpr/ppermute | solution.py:29
  934.2 23.7 %collective-permute-start.6 = (bf16[1,128,128]{1,2,0:T(8,128)(2,1)S(1)}, bf16[1,128,128]{1,2,0:T(8,128)(2,1)S(1)}, u32[]{:S(2)}, u32[]{:S(2)}) collective-permute-start(bf16[1,128,128]{1,2,0:T(8,128)(2,1)S(1)} %fusion.357), channel_id=1, source_target_pairs={{64,0},{128,64},{192,128},{256,192},{320,256},{384,320},{448,384},... | collective-permute-start | bytes 98312 | tf_op jit(solution)/shard_map/while/body/eval_jaxpr/ppermute | solution.py:30
  963.6 45.8 %reduce-scatter.6.cloned.1.call-start = ((), (), s32[]{:S(2)}) async-start(), calls=%async_computation.4 | async-start | bytes 163840 | tf_op jit(solution)/shard_map/while
  1011.2 29.2 %collective-permute-start.7 = (bf16[128,128]{0,1:T(8,128)(2,1)S(1)}, bf16[128,128]{0,1:T(8,128)(2,1)S(1)}, u32[]{:S(2)}, u32[]{:S(2)}) collective-permute-start(bf16[128,128]{0,1:T(8,128)(2,1)S(1)} %convert_select_fusion.2), channel_id=1, source_target_pairs={{0,64},{64,0},{128,192},{192,128},{256,320},{320,256},{384,448},{4... | collective-permute-start | bytes 98312 | tf_op jit(solution)/shard_map/while/body/eval_jaxpr/ppermute | solution.py:19
  1024.9 25.5 %collective-permute-start.5 = (bf16[1,128,128]{1,2,0:T(8,128)(2,1)S(1)}, bf16[1,128,128]{1,2,0:T(8,128)(2,1)S(1)}, u32[]{:S(2)}, u32[]{:S(2)}) collective-permute-start(bf16[1,128,128]{1,2,0:T(8,128)(2,1)S(1)} %fusion.357), channel_id=1, source_target_pairs={{0,64},{64,128},{128,192},{192,256},{256,320},{320,384},{384,448},... | collective-permute-start | bytes 98312 | tf_op jit(solution)/shard_map/while/body/eval_jaxpr/ppermute | solution.py:29
  1026.8 23.6 %collective-permute-start.6 = (bf16[1,128,128]{1,2,0:T(8,128)(2,1)S(1)}, bf16[1,128,128]{1,2,0:T(8,128)(2,1)S(1)}, u32[]{:S(2)}, u32[]{:S(2)}) collective-permute-start(bf16[1,128,128]{1,2,0:T(8,128)(2,1)S(1)} %fusion.357), channel_id=1, source_target_pairs={{64,0},{128,64},{192,128},{256,192},{320,256},{384,320},{448,384},... | collective-permute-start | bytes 98312 | tf_op jit(solution)/shard_map/while/body/eval_jaxpr/ppermute | solution.py:30
  1056.2 46.7 %reduce-scatter.6.cloned.1.call-start = ((), (), s32[]{:S(2)}) async-start(), calls=%async_computation.4 | async-start | bytes 163840 | tf_op jit(solution)/shard_map/while
  1104.6 29.2 %collective-permute-start.7 = (bf16[128,128]{0,1:T(8,128)(2,1)S(1)}, bf16[128,128]{0,1:T(8,128)(2,1)S(1)}, u32[]{:S(2)}, u32[]{:S(2)}) collective-permute-start(bf16[128,128]{0,1:T(8,128)(2,1)S(1)} %convert_select_fusion.2), channel_id=1, source_target_pairs={{0,64},{64,0},{128,192},{192,128},{256,320},{320,256},{384,448},{4... | collective-permute-start | bytes 98312 | tf_op jit(solution)/shard_map/while/body/eval_jaxpr/ppermute | solution.py:19
  1118.3 25.6 %collective-permute-start.5 = (bf16[1,128,128]{1,2,0:T(8,128)(2,1)S(1)}, bf16[1,128,128]{1,2,0:T(8,128)(2,1)S(1)}, u32[]{:S(2)}, u32[]{:S(2)}) collective-permute-start(bf16[1,128,128]{1,2,0:T(8,128)(2,1)S(1)} %fusion.357), channel_id=1, source_target_pairs={{0,64},{64,128},{128,192},{192,256},{256,320},{320,384},{384,448},... | collective-permute-start | bytes 98312 | tf_op jit(solution)/shard_map/while/body/eval_jaxpr/ppermute | solution.py:29
  1120.2 23.6 %collective-permute-start.6 = (bf16[1,128,128]{1,2,0:T(8,128)(2,1)S(1)}, bf16[1,128,128]{1,2,0:T(8,128)(2,1)S(1)}, u32[]{:S(2)}, u32[]{:S(2)}) collective-permute-start(bf16[1,128,128]{1,2,0:T(8,128)(2,1)S(1)} %fusion.357), channel_id=1, source_target_pairs={{64,0},{128,64},{192,128},{256,192},{320,256},{384,320},{448,384},... | collective-permute-start | bytes 98312 | tf_op jit(solution)/shard_map/while/body/eval_jaxpr/ppermute | solution.py:30
  1149.6 46.6 %reduce-scatter.6.cloned.1.call-start = ((), (), s32[]{:S(2)}) async-start(), calls=%async_computation.4 | async-start | bytes 163840 | tf_op jit(solution)/shard_map/while
  1197.9 29.2 %collective-permute-start.7 = (bf16[128,128]{0,1:T(8,128)(2,1)S(1)}, bf16[128,128]{0,1:T(8,128)(2,1)S(1)}, u32[]{:S(2)}, u32[]{:S(2)}) collective-permute-start(bf16[128,128]{0,1:T(8,128)(2,1)S(1)} %convert_select_fusion.2), channel_id=1, source_target_pairs={{0,64},{64,0},{128,192},{192,128},{256,320},{320,256},{384,448},{4... | collective-permute-start | bytes 98312 | tf_op jit(solution)/shard_map/while/body/eval_jaxpr/ppermute | solution.py:19
  1211.6 25.5 %collective-permute-start.5 = (bf16[1,128,128]{1,2,0:T(8,128)(2,1)S(1)}, bf16[1,128,128]{1,2,0:T(8,128)(2,1)S(1)}, u32[]{:S(2)}, u32[]{:S(2)}) collective-permute-start(bf16[1,128,128]{1,2,0:T(8,128)(2,1)S(1)} %fusion.357), channel_id=1, source_target_pairs={{0,64},{64,128},{128,192},{192,256},{256,320},{320,384},{384,448},... | collective-permute-start | bytes 98312 | tf_op jit(solution)/shard_map/while/body/eval_jaxpr/ppermute | solution.py:29
  1213.5 23.6 %collective-permute-start.6 = (bf16[1,128,128]{1,2,0:T(8,128)(2,1)S(1)}, bf16[1,128,128]{1,2,0:T(8,128)(2,1)S(1)}, u32[]{:S(2)}, u32[]{:S(2)}) collective-permute-start(bf16[1,128,128]{1,2,0:T(8,128)(2,1)S(1)} %fusion.357), channel_id=1, source_target_pairs={{64,0},{128,64},{192,128},{256,192},{320,256},{384,320},{448,384},... | collective-permute-start | bytes 98312 | tf_op jit(solution)/shard_map/while/body/eval_jaxpr/ppermute | solution.py:30
  1243.0 45.8 %reduce-scatter.6.cloned.1.call-start = ((), (), s32[]{:S(2)}) async-start(), calls=%async_computation.4 | async-start | bytes 163840 | tf_op jit(solution)/shard_map/while
  1290.5 29.2 %collective-permute-start.7 = (bf16[128,128]{0,1:T(8,128)(2,1)S(1)}, bf16[128,128]{0,1:T(8,128)(2,1)S(1)}, u32[]{:S(2)}, u32[]{:S(2)}) collective-permute-start(bf16[128,128]{0,1:T(8,128)(2,1)S(1)} %convert_select_fusion.2), channel_id=1, source_target_pairs={{0,64},{64,0},{128,192},{192,128},{256,320},{320,256},{384,448},{4... | collective-permute-start | bytes 98312 | tf_op jit(solution)/shard_map/while/body/eval_jaxpr/ppermute | solution.py:19
  1304.2 25.5 %collective-permute-start.5 = (bf16[1,128,128]{1,2,0:T(8,128)(2,1)S(1)}, bf16[1,128,128]{1,2,0:T(8,128)(2,1)S(1)}, u32[]{:S(2)}, u32[]{:S(2)}) collective-permute-start(bf16[1,128,128]{1,2,0:T(8,128)(2,1)S(1)} %fusion.357), channel_id=1, source_target_pairs={{0,64},{64,128},{128,192},{192,256},{256,320},{320,384},{384,448},... | collective-permute-start | bytes 98312 | tf_op jit(solution)/shard_map/while/body/eval_jaxpr/ppermute | solution.py:29
  1306.1 23.6 %collective-permute-start.6 = (bf16[1,128,128]{1,2,0:T(8,128)(2,1)S(1)}, bf16[1,128,128]{1,2,0:T(8,128)(2,1)S(1)}, u32[]{:S(2)}, u32[]{:S(2)}) collective-permute-start(bf16[1,128,128]{1,2,0:T(8,128)(2,1)S(1)} %fusion.357), channel_id=1, source_target_pairs={{64,0},{128,64},{192,128},{256,192},{320,256},{384,320},{448,384},... | collective-permute-start | bytes 98312 | tf_op jit(solution)/shard_map/while/body/eval_jaxpr/ppermute | solution.py:30
  1335.5 46.6 %reduce-scatter.6.cloned.1.call-start = ((), (), s32[]{:S(2)}) async-start(), calls=%async_computation.4 | async-start | bytes 163840 | tf_op jit(solution)/shard_map/while
  1383.7 29.2 %collective-permute-start.7 = (bf16[128,128]{0,1:T(8,128)(2,1)S(1)}, bf16[128,128]{0,1:T(8,128)(2,1)S(1)}, u32[]{:S(2)}, u32[]{:S(2)}) collective-permute-start(bf16[128,128]{0,1:T(8,128)(2,1)S(1)} %convert_select_fusion.2), channel_id=1, source_target_pairs={{0,64},{64,0},{128,192},{192,128},{256,320},{320,256},{384,448},{4... | collective-permute-start | bytes 98312 | tf_op jit(solution)/shard_map/while/body/eval_jaxpr/ppermute | solution.py:19
  1397.4 25.6 %collective-permute-start.5 = (bf16[1,128,128]{1,2,0:T(8,128)(2,1)S(1)}, bf16[1,128,128]{1,2,0:T(8,128)(2,1)S(1)}, u32[]{:S(2)}, u32[]{:S(2)}) collective-permute-start(bf16[1,128,128]{1,2,0:T(8,128)(2,1)S(1)} %fusion.357), channel_id=1, source_target_pairs={{0,64},{64,128},{128,192},{192,256},{256,320},{320,384},{384,448},... | collective-permute-start | bytes 98312 | tf_op jit(solution)/shard_map/while/body/eval_jaxpr/ppermute | solution.py:29
  1399.4 23.6 %collective-permute-start.6 = (bf16[1,128,128]{1,2,0:T(8,128)(2,1)S(1)}, bf16[1,128,128]{1,2,0:T(8,128)(2,1)S(1)}, u32[]{:S(2)}, u32[]{:S(2)}) collective-permute-start(bf16[1,128,128]{1,2,0:T(8,128)(2,1)S(1)} %fusion.357), channel_id=1, source_target_pairs={{64,0},{128,64},{192,128},{256,192},{320,256},{384,320},{448,384},... | collective-permute-start | bytes 98312 | tf_op jit(solution)/shard_map/while/body/eval_jaxpr/ppermute | solution.py:30
  1428.8 44.9 %reduce-scatter.6.cloned.1.call-start = ((), (), s32[]{:S(2)}) async-start(), calls=%async_computation.4 | async-start | bytes 163840 | tf_op jit(solution)/shard_map/while
  1475.4 29.2 %collective-permute-start.7 = (bf16[128,128]{0,1:T(8,128)(2,1)S(1)}, bf16[128,128]{0,1:T(8,128)(2,1)S(1)}, u32[]{:S(2)}, u32[]{:S(2)}) collective-permute-start(bf16[128,128]{0,1:T(8,128)(2,1)S(1)} %convert_select_fusion.2), channel_id=1, source_target_pairs={{0,64},{64,0},{128,192},{192,128},{256,320},{320,256},{384,448},{4... | collective-permute-start | bytes 98312 | tf_op jit(solution)/shard_map/while/body/eval_jaxpr/ppermute | solution.py:19
  1489.1 25.5 %collective-permute-start.5 = (bf16[1,128,128]{1,2,0:T(8,128)(2,1)S(1)}, bf16[1,128,128]{1,2,0:T(8,128)(2,1)S(1)}, u32[]{:S(2)}, u32[]{:S(2)}) collective-permute-start(bf16[1,128,128]{1,2,0:T(8,128)(2,1)S(1)} %fusion.357), channel_id=1, source_target_pairs={{0,64},{64,128},{128,192},{192,256},{256,320},{320,384},{384,448},... | collective-permute-start | bytes 98312 | tf_op jit(solution)/shard_map/while/body/eval_jaxpr/ppermute | solution.py:29
  1491.0 23.6 %collective-permute-start.6 = (bf16[1,128,128]{1,2,0:T(8,128)(2,1)S(1)}, bf16[1,128,128]{1,2,0:T(8,128)(2,1)S(1)}, u32[]{:S(2)}, u32[]{:S(2)}) collective-permute-start(bf16[1,128,128]{1,2,0:T(8,128)(2,1)S(1)} %fusion.357), channel_id=1, source_target_pairs={{64,0},{128,64},{192,128},{256,192},{320,256},{384,320},{448,384},... | collective-permute-start | bytes 98312 | tf_op jit(solution)/shard_map/while/body/eval_jaxpr/ppermute | solution.py:30
  1520.4 102.8 %all-gather.5.cloned.1.call-start = ((), (), s32[]{:S(2)}) async-start(), calls=%async_computation.3 | async-start | bytes 4456448 | tf_op jit(solution)/shard_map/all_gather | solution.py:324
  1522.8 14.4 all-to-all-start
  1628.0 18.6 %collective-permute-start.13 = (bf16[8,27,512]{2,1,0:T(8,128)(2,1)S(1)}, bf16[8,27,512]{2,1,0:T(8,128)(2,1)S(1)}, u32[]{:S(2)}, u32[]{:S(2)}) collective-permute-start(bf16[8,27,512]{2,1,0:T(8,128)(2,1)S(1)} %pad_maximum_fusion.3), channel_id=1, source_target_pairs={{0,64},{64,0},{128,192},{192,128},{256,320},{320,256},{384,448},{4... | collective-permute-start | bytes 663560 | tf_op jit(solution)/shard_map/ppermute | solution.py:19
  (87 other events, 1684.2 us)
Sparse Core Ops, SparseCore 0:
  62.8 128.8 all-gather.2
  786.4 37.1 reduce-scatter.5
  881.2 35.7 reduce-scatter.5
  991.8 17.6 reduce-scatter.5
  1067.1 35.7 reduce-scatter.5
  1160.4 35.7 reduce-scatter.5
  1271.2 17.5 reduce-scatter.5
  1346.3 35.7 reduce-scatter.5
  1439.6 33.9 reduce-scatter.5
  1523.0 100.1 all-gather.4
where the time goes:
time: 1680 us; the launch traced here: 1670 us
  waiting for transfers between devices  607 us (36%)
  starting transfers between devices  570 us (34%)
  local copies, waits for them, and re-layouts  177 us (11%)
  loops' own time  125 us (7%)
  blocking collectives  86.9 us (5%)
  other arithmetic  74.3 us (4%)
  matrix products  19 us (1%)
    ppermute x54, starting transfers between devices, from_partner(): return lax.ppermute(block, axis, route)  323 us
    while x16, waiting for transfers between devices  245 us
    ppermute x16, starting transfers between devices, with_halo(): after = lax.ppermute(first, axis, down)  175 us
    ppermute x54, waiting for transfers between devices, from_partner(): return lax.ppermute(block, axis, route)  156 us
    all_gather x1, waiting for transfers between devices, on_device(): lane_kernels = lax.all_gather(lane_shares, 'dp', axis=1, tiled=True)  129 us
    all_gather x8, blocking collectives, channel_gather(): return lax.all_gather(source, 'chan', axis=0, tiled=True)  86.9 us
    ppermute x16, starting transfers between devices, with_halo(): before = lax.ppermute(last, axis, up)  67.9 us
    another operation x1, loops' own time, on_device(): lax.fori_loop(0, tick_count, forward_tick, (empty_rows, empty_slots, empt...  67.6 us
  transfers between devices with their start and end apart: 97, of which 52 were waited for; matrix products, arithmetic and copies ran while one was open for 3% of the time, Pallas kernels for 0%

commit v1 on v0

--- a/solution.py
+++ b/solution.py
@@ -154,7 +154,9 @@
 
 
 def channel_gather(source):
-    return lax.all_gather(source, "chan", axis=0, tiled=True)
+    return jnp.concatenate(
+        lax.all_to_all(jnp.stack([source] * lax.axis_size("chan")), "chan", 0, 0), axis=0
+    )
 
 
 def section_rims(source):

time: 1680 us -> 1610 us (0.958)
  blocking collectives: 86.9 us -> 0 us
  starting transfers between devices: 570 us -> 593 us
  waiting for transfers between devices: 607 us -> 590 us
    all_gather x8 -> x0, blocking collectives: 86.9 us -> none  [channel_gather(): return lax.all_gather(source, 'chan', axis=0, tiled=True)]
    all_to_all x0 -> x8, starting transfers between devices: none -> 27.6 us  [channel_gather(): lax.all_to_all(jnp.stack([source] * lax.axis_size('chan')), 'chan', 0, 0)]
    ppermute x54, waiting for transfers between devices: 156 us -> 130 us  [from_partner(): return lax.ppermute(block, axis, route)]
  transfers between devices with their start and end apart: 97 -> 105, of which waited for: 52 -> 58; matrix products, arithmetic and copies ran while one was open for 3% -> 3% of each run, Pallas kernels for 0% -> 0%
where the time goes in v1:
time: 1610 us; the launch traced here: 1600 us
  starting transfers between devices  593 us (37%)
  waiting for transfers between devices  590 us (37%)
  local copies, waits for them, and re-layouts  182 us (11%)
  loops' own time  119 us (7%)
  other arithmetic  79.6 us (5%)
  matrix products  21.4 us (1%)
    ppermute x54, starting transfers between devices, from_partner(): return lax.ppermute(block, axis, route)  317 us
    while x16, waiting for transfers between devices  252 us
    ppermute x16, starting transfers between devices, with_halo(): after = lax.ppermute(first, axis, down)  178 us
    ppermute x54, waiting for transfers between devices, from_partner(): return lax.ppermute(block, axis, route)  130 us
    all_gather x1, waiting for transfers between devices, on_device(): lane_kernels = lax.all_gather(lane_shares, 'dp', axis=1, tiled=True)  129 us
    ppermute x16, starting transfers between devices, with_halo(): before = lax.ppermute(last, axis, up)  66.9 us
    another operation x1, loops' own time, on_device(): lax.fori_loop(0, tick_count, forward_tick, (empty_rows, empty_slots, empt...  65.8 us
    another operation x1, loops' own time, on_device(): lax.fori_loop(0, tick_count, backward_tick, (empty_rows, empty_slots, emp...  51.5 us
  transfers between devices with their start and end apart: 105, of which 58 were waited for; matrix products, arithmetic and copies ran while one was open for 3% of the time, Pallas kernels for 0%

profile of v1, /device:TPU:8, one launch (start us, length us, event | category | flops | bytes accessed | tf_op | source)
XLA Modules:
  0.0 1599.1 jit_solution(17969269928388429419)
XLA Ops:
  6.5 15.7 collective-permute-start.10
  22.3 5.9 collective-permute-done.10
  49.9 6.5 pad_maximum_fusion.2
  56.3 6.4 copy.1518
  62.8 129.0 %all-gather.3.cloned.1.call-done = bf16[2,128,27,512]{3,0,2,1:T(2,128)(2,1)} async-done(((bf16[2,8,27,512]{3,0,2,1:T(2,128)(2,1)}), bf16[2,128,27,512]{3,0,2,1:T(2,128)(2,1)}) %all-gather.3.cloned.1.call-update) | async-done | bytes 7077904 | tf_op jit(solution)/shard_map/all_gather | solution.py:216
  191.8 15.4 fusion.313
  207.2 14.8 copy.1589
  226.2 14.8 copy.1590
  245.3 455.0 %while.42 = (s32[]{:T(128)}, bf16[2,128,128]{1,2,0:T(8,128)(2,1)S(1)}, bf16[2,1,128,128]{2,3,1,0:T(8,128)(2,1)S(1)}, bf16[2,1,128,128]{2,3,1,0:T(8,128)(2,1)S(1)...) while((s32[]{:T(128)}, ...), condition=%wide.region_4.5_spmd, body=%wide.region_0.4_spmd.sunk | while | flops 455368896 | bytes 30984176 | solution.py:268
  264.4 7.0 collective-permute-start.2
  271.4 12.7 collective-permute-start
  292.2 8.9 collective-permute-start.4
  320.6 8.3 collective-permute-start.2
  328.9 8.6 collective-permute-start
  337.4 6.0 collective-permute-start.1
  343.4 9.1 collective-permute-start.3
  386.5 8.9 collective-permute-start
  395.4 5.7 collective-permute-start.1
  431.8 18.7 %collective-permute-start.2 = (bf16[128,128]{0,1:T(8,128)(2,1)S(1)}, bf16[128,128]{0,1:T(8,128)(2,1)S(1)}, u32[]{:S(2)}, u32[]{:S(2)}) collective-permute-start(bf16[128,128]{0,1:T(8,128)(2,1)S(1)} %broadcast_select_fusion.4), channel_id=1, source_target_pairs={{0,64},{64,0},{128,192},{192,128},{256,320},{320,256},{384,448},{4... | collective-permute-start | bytes 98312 | tf_op jit(solution)/shard_map/while/body/eval_jaxpr/ppermute | solution.py:19
  452.5 12.6 collective-permute-start.1
  495.8 8.0 collective-permute-start.2
  503.9 6.0 collective-permute-start
  509.9 8.6 collective-permute-start.1
  556.6 6.6 collective-permute-start
  563.2 8.0 collective-permute-start.1
  577.0 9.7 collective-permute-start.4
  606.2 8.9 collective-permute-start.2
  615.1 7.7 collective-permute-start
  622.8 6.9 collective-permute-start.1
  629.7 7.1 collective-permute-start.3
  667.6 17.3 %collective-permute-start = (bf16[1,128,128]{1,2,0:T(8,128)(2,1)S(1)}, bf16[1,128,128]{1,2,0:T(8,128)(2,1)S(1)}, u32[]{:S(2)}, u32[]{:S(2)}) collective-permute-start(bf16[1,128,128]{1,2,0:T(8,128)(2,1)S(1)} %fusion.355), channel_id=1, source_target_pairs={{64,0},{128,64},{192,128},{256,192},{320,256},{384,320},{448,384},... | collective-permute-start | bytes 98312 | tf_op jit(solution)/shard_map/while/body/eval_jaxpr/ppermute | solution.py:30
  702.3 748.0 %while.43 = (s32[]{:T(128)}, bf16[2,128,128]{1,2,0:T(8,128)(2,1)}, bf16[2,1,128,128]{2,3,1,0:T(8,128)(2,1)}, bf16[2,1,128,128]{2,3,1,0:T(8,128)(2,1)}, s32[2]{0:...) while((s32[]{:T(128)}, bf16[2,128,128]{1,2,0:T(8,128)(2,1)}, ...), condition=%wide.region_10.11_spmd, body=%wide.region_5.10_spmd.sunk | while | flops 454528576 | bytes 34589428 | solution.py:321
  713.4 41.7 %reduce-scatter.6.cloned.1.call-done = bf16[128,128]{1,0:T(8,128)(2,1)} async-done(((bf16[512,128]{1,0:T(8,128)(2,1)}), bf16[128,128]{1,0:T(8,128)(2,1)}) %reduce-scatter.6.cloned.1.call-update) | async-done | bytes 32784 | tf_op jit(solution)/shard_map/while
  756.8 12.8 collective-permute-start.7
  772.4 13.5 collective-permute-start.6
  812.8 35.2 %reduce-scatter.6.cloned.1.call-done = bf16[128,128]{1,0:T(8,128)(2,1)} async-done(((bf16[512,128]{1,0:T(8,128)(2,1)}), bf16[128,128]{1,0:T(8,128)(2,1)}) %reduce-scatter.6.cloned.1.call-update) | async-done | bytes 32784 | tf_op jit(solution)/shard_map/while
  849.7 12.8 collective-permute-start.7
  865.3 13.5 collective-permute-start.6
  904.2 17.4 %conditional.5 = (bf16[512,128]{0,1:T(8,128)(2,1)S(1)}) conditional(s32[]{:T(128)} %clamp.25, () %tuple.351, (bf16[128,128]{0,1:T(8,128)(2,1)S(1)}, bf16[3,128,4608]{2,1,0:T(8,128)(2,1)}) %tuple.352, (bf16[128,128]{0,1:T(8,128)(2,1)S(1)}, bf16[3,128,4608]{2,1,0:T(8,128)(2,1)}) %tuple.353), branch_computations={%region_6.6_spmd, %region_7.7_spmd, %region_8.8_spmd} | conditional | flops 453791232 | bytes 30786196 | solution.py:302
  923.0 17.7 %reduce-scatter.6.cloned.1.call-done = bf16[128,128]{1,0:T(8,128)(2,1)} async-done(((bf16[512,128]{1,0:T(8,128)(2,1)}), bf16[128,128]{1,0:T(8,128)(2,1)}) %reduce-scatter.6.cloned.1.call-update) | async-done | bytes 32784 | tf_op jit(solution)/shard_map/while
  942.4 12.8 collective-permute-start.7
  958.1 13.5 collective-permute-start.6
  998.4 35.2 %reduce-scatter.6.cloned.1.call-done = bf16[128,128]{1,0:T(8,128)(2,1)} async-done(((bf16[512,128]{1,0:T(8,128)(2,1)}), bf16[128,128]{1,0:T(8,128)(2,1)}) %reduce-scatter.6.cloned.1.call-update) | async-done | bytes 32784 | tf_op jit(solution)/shard_map/while
  1035.4 12.8 collective-permute-start.7
  1051.0 13.5 collective-permute-start.6
  1091.3 35.2 %reduce-scatter.6.cloned.1.call-done = bf16[128,128]{1,0:T(8,128)(2,1)} async-done(((bf16[512,128]{1,0:T(8,128)(2,1)}), bf16[128,128]{1,0:T(8,128)(2,1)}) %reduce-scatter.6.cloned.1.call-update) | async-done | bytes 32784 | tf_op jit(solution)/shard_map/while
  1128.3 12.8 collective-permute-start.7
  1143.9 13.5 collective-permute-start.6
  1182.8 17.4 %conditional.5 = (bf16[512,128]{0,1:T(8,128)(2,1)S(1)}) conditional(s32[]{:T(128)} %clamp.25, () %tuple.351, (bf16[128,128]{0,1:T(8,128)(2,1)S(1)}, bf16[3,128,4608]{2,1,0:T(8,128)(2,1)}) %tuple.352, (bf16[128,128]{0,1:T(8,128)(2,1)S(1)}, bf16[3,128,4608]{2,1,0:T(8,128)(2,1)}) %tuple.353), branch_computations={%region_6.6_spmd, %region_7.7_spmd, %region_8.8_spmd} | conditional | flops 453791232 | bytes 30786196 | solution.py:302
  1201.6 17.7 %reduce-scatter.6.cloned.1.call-done = bf16[128,128]{1,0:T(8,128)(2,1)} async-done(((bf16[512,128]{1,0:T(8,128)(2,1)}), bf16[128,128]{1,0:T(8,128)(2,1)}) %reduce-scatter.6.cloned.1.call-update) | async-done | bytes 32784 | tf_op jit(solution)/shard_map/while
  1221.0 12.8 collective-permute-start.7
  1236.6 13.5 collective-permute-start.6
  1276.9 35.4 %reduce-scatter.6.cloned.1.call-done = bf16[128,128]{1,0:T(8,128)(2,1)} async-done(((bf16[512,128]{1,0:T(8,128)(2,1)}), bf16[128,128]{1,0:T(8,128)(2,1)}) %reduce-scatter.6.cloned.1.call-update) | async-done | bytes 32784 | tf_op jit(solution)/shard_map/while
  1314.0 12.8 collective-permute-start.7
  1329.6 13.5 collective-permute-start.6
  1369.9 33.7 %reduce-scatter.6.cloned.1.call-done = bf16[128,128]{1,0:T(8,128)(2,1)} async-done(((bf16[512,128]{1,0:T(8,128)(2,1)}), bf16[128,128]{1,0:T(8,128)(2,1)}) %reduce-scatter.6.cloned.1.call-update) | async-done | bytes 32784 | tf_op jit(solution)/shard_map/while
  1405.3 12.8 collective-permute-start.7
  1420.9 13.5 collective-permute-start.6
  1456.4 10.8 all-to-all-done.1
  1487.3 50.0 %all-gather.5.cloned.1.call-done = bf16[2,1,512,2048]{3,2,1,0:T(8,128)(2,1)} async-done(((bf16[2,1,512,128]{3,2,1,0:T(8,128)(2,1)}), bf16[2,1,512,2048]{3,2,1,0:T(8,128)(2,1)}) %all-gather.5.cloned.1.call-update) | async-done | bytes 4194320 | tf_op jit(solution)/shard_map/all_gather | solution.py:326
  1543.3 9.9 collective-permute-start.13
  1554.1 16.1 %collective-permute-done.13 = bf16[8,27,512]{2,1,0:T(8,128)(2,1)S(1)} collective-permute-done((bf16[8,27,512]{2,1,0:T(8,128)(2,1)S(1)}, bf16[8,27,512]{2,1,0:T(8,128)(2,1)S(1)}, u32[]{:S(2)}, u32[]{:S(2)}) %collective-permute-start.13) | collective-permute-done | bytes 221216 | tf_op jit(solution)/shard_map/ppermute | solution.py:19
  1573.3 6.9 collective-permute-done.14
  1585.1 5.8 collective-permute-done.15
  (920 shorter events, 504.9 us)
Async XLA Ops:
  6.5 185.2 %all-gather.3.cloned.1.call-start = ((), (), s32[]{:S(2)}) async-start(), calls=%async_computation.3 | async-start | bytes 7520256 | tf_op jit(solution)/shard_map/all_gather | solution.py:216
  6.5 21.6 %collective-permute-start.10 = (bf16[8,27,512]{2,0,1:T(8,128)(2,1)}, bf16[8,27,512]{2,0,1:T(8,128)(2,1)S(1)}, u32[]{:S(2)}, u32[]{:S(2)}) collective-permute-start(bf16[8,27,512]{2,0,1:T(8,128)(2,1)} %bitcast.641), channel_id=1, source_target_pairs={{0,64},{64,0},{128,192},{192,128},{256,320},{320,256},{384,448},{4... | collective-permute-start | bytes 663560 | tf_op jit(solution)/shard_map/ppermute | solution.py:19
  264.4 21.7 %collective-permute-start.2 = (bf16[128,128]{0,1:T(8,128)(2,1)S(1)}, bf16[128,128]{0,1:T(8,128)(2,1)S(1)}, u32[]{:S(2)}, u32[]{:S(2)}) collective-permute-start(bf16[128,128]{0,1:T(8,128)(2,1)S(1)} %broadcast_select_fusion.4), channel_id=1, source_target_pairs={{0,64},{64,0},{128,192},{192,128},{256,320},{320,256},{384,448},{4... | collective-permute-start | bytes 98312 | tf_op jit(solution)/shard_map/while/body/eval_jaxpr/ppermute | solution.py:19
  271.4 29.7 %collective-permute-start = (bf16[1,128,128]{1,2,0:T(8,128)(2,1)S(1)}, bf16[1,128,128]{1,2,0:T(8,128)(2,1)S(1)}, u32[]{:S(2)}, u32[]{:S(2)}) collective-permute-start(bf16[1,128,128]{1,2,0:T(8,128)(2,1)S(1)} %fusion.355), channel_id=1, source_target_pairs={{64,0},{128,64},{192,128},{256,192},{320,256},{384,320},{448,384},... | collective-permute-start | bytes 98312 | tf_op jit(solution)/shard_map/while/body/eval_jaxpr/ppermute | solution.py:30
  284.1 17.0 %collective-permute-start.1 = (bf16[1,128,128]{1,2,0:T(8,128)(2,1)S(1)}, bf16[1,128,128]{1,2,0:T(8,128)(2,1)S(1)}, u32[]{:S(2)}, u32[]{:S(2)}) collective-permute-start(bf16[1,128,128]{1,2,0:T(8,128)(2,1)S(1)} %fusion.355), channel_id=1, source_target_pairs={{0,64},{64,128},{128,192},{192,256},{256,320},{320,384},{384,448},... | collective-permute-start | bytes 98312 | tf_op jit(solution)/shard_map/while/body/eval_jaxpr/ppermute | solution.py:29
  292.2 10.8 collective-permute-start.4
  320.6 22.9 %collective-permute-start.2 = (bf16[128,128]{0,1:T(8,128)(2,1)S(1)}, bf16[128,128]{0,1:T(8,128)(2,1)S(1)}, u32[]{:S(2)}, u32[]{:S(2)}) collective-permute-start(bf16[128,128]{0,1:T(8,128)(2,1)S(1)} %broadcast_select_fusion.4), channel_id=1, source_target_pairs={{0,64},{64,0},{128,192},{192,128},{256,320},{320,256},{384,448},{4... | collective-permute-start | bytes 98312 | tf_op jit(solution)/shard_map/while/body/eval_jaxpr/ppermute | solution.py:19
  328.9 27.5 %collective-permute-start = (bf16[1,128,128]{1,2,0:T(8,128)(2,1)S(1)}, bf16[1,128,128]{1,2,0:T(8,128)(2,1)S(1)}, u32[]{:S(2)}, u32[]{:S(2)}) collective-permute-start(bf16[1,128,128]{1,2,0:T(8,128)(2,1)S(1)} %fusion.355), channel_id=1, source_target_pairs={{64,0},{128,64},{192,128},{256,192},{320,256},{384,320},{448,384},... | collective-permute-start | bytes 98312 | tf_op jit(solution)/shard_map/while/body/eval_jaxpr/ppermute | solution.py:30
  337.4 18.9 %collective-permute-start.1 = (bf16[1,128,128]{1,2,0:T(8,128)(2,1)S(1)}, bf16[1,128,128]{1,2,0:T(8,128)(2,1)S(1)}, u32[]{:S(2)}, u32[]{:S(2)}) collective-permute-start(bf16[1,128,128]{1,2,0:T(8,128)(2,1)S(1)} %fusion.355), channel_id=1, source_target_pairs={{0,64},{64,128},{128,192},{192,256},{256,320},{320,384},{384,448},... | collective-permute-start | bytes 98312 | tf_op jit(solution)/shard_map/while/body/eval_jaxpr/ppermute | solution.py:29
  343.4 11.0 collective-permute-start.3
  384.5 16.5 %collective-permute-start.2 = (bf16[128,128]{0,1:T(8,128)(2,1)S(1)}, bf16[128,128]{0,1:T(8,128)(2,1)S(1)}, u32[]{:S(2)}, u32[]{:S(2)}) collective-permute-start(bf16[128,128]{0,1:T(8,128)(2,1)S(1)} %broadcast_select_fusion.4), channel_id=1, source_target_pairs={{0,64},{64,0},{128,192},{192,128},{256,320},{320,256},{384,448},{4... | collective-permute-start | bytes 98312 | tf_op jit(solution)/shard_map/while/body/eval_jaxpr/ppermute | solution.py:19
  386.5 23.9 %collective-permute-start = (bf16[1,128,128]{1,2,0:T(8,128)(2,1)S(1)}, bf16[1,128,128]{1,2,0:T(8,128)(2,1)S(1)}, u32[]{:S(2)}, u32[]{:S(2)}) collective-permute-start(bf16[1,128,128]{1,2,0:T(8,128)(2,1)S(1)} %fusion.355), channel_id=1, source_target_pairs={{64,0},{128,64},{192,128},{256,192},{320,256},{384,320},{448,384},... | collective-permute-start | bytes 98312 | tf_op jit(solution)/shard_map/while/body/eval_jaxpr/ppermute | solution.py:30
  395.4 15.4 collective-permute-start.1
  431.8 33.3 %collective-permute-start.2 = (bf16[128,128]{0,1:T(8,128)(2,1)S(1)}, bf16[128,128]{0,1:T(8,128)(2,1)S(1)}, u32[]{:S(2)}, u32[]{:S(2)}) collective-permute-start(bf16[128,128]{0,1:T(8,128)(2,1)S(1)} %broadcast_select_fusion.4), channel_id=1, source_target_pairs={{0,64},{64,0},{128,192},{192,128},{256,320},{320,256},{384,448},{4... | collective-permute-start | bytes 98312 | tf_op jit(solution)/shard_map/while/body/eval_jaxpr/ppermute | solution.py:19
  450.5 22.3 %collective-permute-start = (bf16[1,128,128]{1,2,0:T(8,128)(2,1)S(1)}, bf16[1,128,128]{1,2,0:T(8,128)(2,1)S(1)}, u32[]{:S(2)}, u32[]{:S(2)}) collective-permute-start(bf16[1,128,128]{1,2,0:T(8,128)(2,1)S(1)} %fusion.355), channel_id=1, source_target_pairs={{64,0},{128,64},{192,128},{256,192},{320,256},{384,320},{448,384},... | collective-permute-start | bytes 98312 | tf_op jit(solution)/shard_map/while/body/eval_jaxpr/ppermute | solution.py:30
  452.5 20.4 %collective-permute-start.1 = (bf16[1,128,128]{1,2,0:T(8,128)(2,1)S(1)}, bf16[1,128,128]{1,2,0:T(8,128)(2,1)S(1)}, u32[]{:S(2)}, u32[]{:S(2)}) collective-permute-start(bf16[1,128,128]{1,2,0:T(8,128)(2,1)S(1)} %fusion.355), channel_id=1, source_target_pairs={{0,64},{64,128},{128,192},{192,256},{256,320},{320,384},{384,448},... | collective-permute-start | bytes 98312 | tf_op jit(solution)/shard_map/while/body/eval_jaxpr/ppermute | solution.py:29
  495.8 22.6 %collective-permute-start.2 = (bf16[128,128]{0,1:T(8,128)(2,1)S(1)}, bf16[128,128]{0,1:T(8,128)(2,1)S(1)}, u32[]{:S(2)}, u32[]{:S(2)}) collective-permute-start(bf16[128,128]{0,1:T(8,128)(2,1)S(1)} %broadcast_select_fusion.4), channel_id=1, source_target_pairs={{0,64},{64,0},{128,192},{192,128},{256,320},{320,256},{384,448},{4... | collective-permute-start | bytes 98312 | tf_op jit(solution)/shard_map/while/body/eval_jaxpr/ppermute | solution.py:19
  503.9 22.3 %collective-permute-start = (bf16[1,128,128]{1,2,0:T(8,128)(2,1)S(1)}, bf16[1,128,128]{1,2,0:T(8,128)(2,1)S(1)}, u32[]{:S(2)}, u32[]{:S(2)}) collective-permute-start(bf16[1,128,128]{1,2,0:T(8,128)(2,1)S(1)} %fusion.355), channel_id=1, source_target_pairs={{64,0},{128,64},{192,128},{256,192},{320,256},{384,320},{448,384},... | collective-permute-start | bytes 98312 | tf_op jit(solution)/shard_map/while/body/eval_jaxpr/ppermute | solution.py:30
  509.9 16.3 %collective-permute-start.1 = (bf16[1,128,128]{1,2,0:T(8,128)(2,1)S(1)}, bf16[1,128,128]{1,2,0:T(8,128)(2,1)S(1)}, u32[]{:S(2)}, u32[]{:S(2)}) collective-permute-start(bf16[1,128,128]{1,2,0:T(8,128)(2,1)S(1)} %fusion.355), channel_id=1, source_target_pairs={{0,64},{64,128},{128,192},{192,256},{256,320},{320,384},{384,448},... | collective-permute-start | bytes 98312 | tf_op jit(solution)/shard_map/while/body/eval_jaxpr/ppermute | solution.py:29
  554.3 16.8 %collective-permute-start.2 = (bf16[128,128]{0,1:T(8,128)(2,1)S(1)}, bf16[128,128]{0,1:T(8,128)(2,1)S(1)}, u32[]{:S(2)}, u32[]{:S(2)}) collective-permute-start(bf16[128,128]{0,1:T(8,128)(2,1)S(1)} %broadcast_select_fusion.4), channel_id=1, source_target_pairs={{0,64},{64,0},{128,192},{192,128},{256,320},{320,256},{384,448},{4... | collective-permute-start | bytes 98312 | tf_op jit(solution)/shard_map/while/body/eval_jaxpr/ppermute | solution.py:19
  556.6 30.1 %collective-permute-start = (bf16[1,128,128]{1,2,0:T(8,128)(2,1)S(1)}, bf16[1,128,128]{1,2,0:T(8,128)(2,1)S(1)}, u32[]{:S(2)}, u32[]{:S(2)}) collective-permute-start(bf16[1,128,128]{1,2,0:T(8,128)(2,1)S(1)} %fusion.355), channel_id=1, source_target_pairs={{64,0},{128,64},{192,128},{256,192},{320,256},{384,320},{448,384},... | collective-permute-start | bytes 98312 | tf_op jit(solution)/shard_map/while/body/eval_jaxpr/ppermute | solution.py:30
  563.2 23.5 %collective-permute-start.1 = (bf16[1,128,128]{1,2,0:T(8,128)(2,1)S(1)}, bf16[1,128,128]{1,2,0:T(8,128)(2,1)S(1)}, u32[]{:S(2)}, u32[]{:S(2)}) collective-permute-start(bf16[1,128,128]{1,2,0:T(8,128)(2,1)S(1)} %fusion.355), channel_id=1, source_target_pairs={{0,64},{64,128},{128,192},{192,256},{256,320},{320,384},{384,448},... | collective-permute-start | bytes 98312 | tf_op jit(solution)/shard_map/while/body/eval_jaxpr/ppermute | solution.py:29
  577.0 11.6 collective-permute-start.4
  606.2 23.5 %collective-permute-start.2 = (bf16[128,128]{0,1:T(8,128)(2,1)S(1)}, bf16[128,128]{0,1:T(8,128)(2,1)S(1)}, u32[]{:S(2)}, u32[]{:S(2)}) collective-permute-start(bf16[128,128]{0,1:T(8,128)(2,1)S(1)} %broadcast_select_fusion.4), channel_id=1, source_target_pairs={{0,64},{64,0},{128,192},{192,128},{256,320},{320,256},{384,448},{4... | collective-permute-start | bytes 98312 | tf_op jit(solution)/shard_map/while/body/eval_jaxpr/ppermute | solution.py:19
  615.1 25.5 %collective-permute-start = (bf16[1,128,128]{1,2,0:T(8,128)(2,1)S(1)}, bf16[1,128,128]{1,2,0:T(8,128)(2,1)S(1)}, u32[]{:S(2)}, u32[]{:S(2)}) collective-permute-start(bf16[1,128,128]{1,2,0:T(8,128)(2,1)S(1)} %fusion.355), channel_id=1, source_target_pairs={{64,0},{128,64},{192,128},{256,192},{320,256},{384,320},{448,384},... | collective-permute-start | bytes 98312 | tf_op jit(solution)/shard_map/while/body/eval_jaxpr/ppermute | solution.py:30
  622.8 17.8 %collective-permute-start.1 = (bf16[1,128,128]{1,2,0:T(8,128)(2,1)S(1)}, bf16[1,128,128]{1,2,0:T(8,128)(2,1)S(1)}, u32[]{:S(2)}, u32[]{:S(2)}) collective-permute-start(bf16[1,128,128]{1,2,0:T(8,128)(2,1)S(1)} %fusion.355), channel_id=1, source_target_pairs={{0,64},{64,128},{128,192},{192,256},{256,320},{320,384},{384,448},... | collective-permute-start | bytes 98312 | tf_op jit(solution)/shard_map/while/body/eval_jaxpr/ppermute | solution.py:29
  663.6 23.2 %collective-permute-start.2 = (bf16[128,128]{0,1:T(8,128)(2,1)S(1)}, bf16[128,128]{0,1:T(8,128)(2,1)S(1)}, u32[]{:S(2)}, u32[]{:S(2)}) collective-permute-start(bf16[128,128]{0,1:T(8,128)(2,1)S(1)} %broadcast_select_fusion.4), channel_id=1, source_target_pairs={{0,64},{64,0},{128,192},{192,128},{256,320},{320,256},{384,448},{4... | collective-permute-start | bytes 98312 | tf_op jit(solution)/shard_map/while/body/eval_jaxpr/ppermute | solution.py:19
  667.6 30.4 %collective-permute-start = (bf16[1,128,128]{1,2,0:T(8,128)(2,1)S(1)}, bf16[1,128,128]{1,2,0:T(8,128)(2,1)S(1)}, u32[]{:S(2)}, u32[]{:S(2)}) collective-permute-start(bf16[1,128,128]{1,2,0:T(8,128)(2,1)S(1)} %fusion.355), channel_id=1, source_target_pairs={{64,0},{128,64},{192,128},{256,192},{320,256},{384,320},{448,384},... | collective-permute-start | bytes 98312 | tf_op jit(solution)/shard_map/while/body/eval_jaxpr/ppermute | solution.py:30
  684.8 15.4 collective-permute-start.1
  702.5 52.6 %reduce-scatter.6.cloned.1.call-start = ((), (), s32[]{:S(2)}) async-start(), calls=%async_computation.5 | async-start | bytes 163840 | tf_op jit(solution)/shard_map/while
  756.8 29.2 %collective-permute-start.7 = (bf16[128,128]{0,1:T(8,128)(2,1)S(1)}, bf16[128,128]{0,1:T(8,128)(2,1)S(1)}, u32[]{:S(2)}, u32[]{:S(2)}) collective-permute-start(bf16[128,128]{0,1:T(8,128)(2,1)S(1)} %convert_select_fusion.2), channel_id=1, source_target_pairs={{0,64},{64,0},{128,192},{192,128},{256,320},{320,256},{384,448},{4... | collective-permute-start | bytes 98312 | tf_op jit(solution)/shard_map/while/body/eval_jaxpr/ppermute | solution.py:19
  770.5 25.6 %collective-permute-start.5 = (bf16[1,128,128]{1,2,0:T(8,128)(2,1)S(1)}, bf16[1,128,128]{1,2,0:T(8,128)(2,1)S(1)}, u32[]{:S(2)}, u32[]{:S(2)}) collective-permute-start(bf16[1,128,128]{1,2,0:T(8,128)(2,1)S(1)} %fusion.361), channel_id=1, source_target_pairs={{0,64},{64,128},{128,192},{192,256},{256,320},{320,384},{384,448},... | collective-permute-start | bytes 98312 | tf_op jit(solution)/shard_map/while/body/eval_jaxpr/ppermute | solution.py:29
  772.4 23.7 %collective-permute-start.6 = (bf16[1,128,128]{1,2,0:T(8,128)(2,1)S(1)}, bf16[1,128,128]{1,2,0:T(8,128)(2,1)S(1)}, u32[]{:S(2)}, u32[]{:S(2)}) collective-permute-start(bf16[1,128,128]{1,2,0:T(8,128)(2,1)S(1)} %fusion.361), channel_id=1, source_target_pairs={{64,0},{128,64},{192,128},{256,192},{320,256},{384,320},{448,384},... | collective-permute-start | bytes 98312 | tf_op jit(solution)/shard_map/while/body/eval_jaxpr/ppermute | solution.py:30
  801.8 46.2 %reduce-scatter.6.cloned.1.call-start = ((), (), s32[]{:S(2)}) async-start(), calls=%async_computation.5 | async-start | bytes 163840 | tf_op jit(solution)/shard_map/while
  849.7 29.2 %collective-permute-start.7 = (bf16[128,128]{0,1:T(8,128)(2,1)S(1)}, bf16[128,128]{0,1:T(8,128)(2,1)S(1)}, u32[]{:S(2)}, u32[]{:S(2)}) collective-permute-start(bf16[128,128]{0,1:T(8,128)(2,1)S(1)} %convert_select_fusion.2), channel_id=1, source_target_pairs={{0,64},{64,0},{128,192},{192,128},{256,320},{320,256},{384,448},{4... | collective-permute-start | bytes 98312 | tf_op jit(solution)/shard_map/while/body/eval_jaxpr/ppermute | solution.py:19
  863.4 25.6 %collective-permute-start.5 = (bf16[1,128,128]{1,2,0:T(8,128)(2,1)S(1)}, bf16[1,128,128]{1,2,0:T(8,128)(2,1)S(1)}, u32[]{:S(2)}, u32[]{:S(2)}) collective-permute-start(bf16[1,128,128]{1,2,0:T(8,128)(2,1)S(1)} %fusion.361), channel_id=1, source_target_pairs={{0,64},{64,128},{128,192},{192,256},{256,320},{320,384},{384,448},... | collective-permute-start | bytes 98312 | tf_op jit(solution)/shard_map/while/body/eval_jaxpr/ppermute | solution.py:29
  865.3 23.7 %collective-permute-start.6 = (bf16[1,128,128]{1,2,0:T(8,128)(2,1)S(1)}, bf16[1,128,128]{1,2,0:T(8,128)(2,1)S(1)}, u32[]{:S(2)}, u32[]{:S(2)}) collective-permute-start(bf16[1,128,128]{1,2,0:T(8,128)(2,1)S(1)} %fusion.361), channel_id=1, source_target_pairs={{64,0},{128,64},{192,128},{256,192},{320,256},{384,320},{448,384},... | collective-permute-start | bytes 98312 | tf_op jit(solution)/shard_map/while/body/eval_jaxpr/ppermute | solution.py:30
  894.7 46.0 %reduce-scatter.6.cloned.1.call-start = ((), (), s32[]{:S(2)}) async-start(), calls=%async_computation.5 | async-start | bytes 163840 | tf_op jit(solution)/shard_map/while
  942.4 29.2 %collective-permute-start.7 = (bf16[128,128]{0,1:T(8,128)(2,1)S(1)}, bf16[128,128]{0,1:T(8,128)(2,1)S(1)}, u32[]{:S(2)}, u32[]{:S(2)}) collective-permute-start(bf16[128,128]{0,1:T(8,128)(2,1)S(1)} %convert_select_fusion.2), channel_id=1, source_target_pairs={{0,64},{64,0},{128,192},{192,128},{256,320},{320,256},{384,448},{4... | collective-permute-start | bytes 98312 | tf_op jit(solution)/shard_map/while/body/eval_jaxpr/ppermute | solution.py:19
  956.1 25.6 %collective-permute-start.5 = (bf16[1,128,128]{1,2,0:T(8,128)(2,1)S(1)}, bf16[1,128,128]{1,2,0:T(8,128)(2,1)S(1)}, u32[]{:S(2)}, u32[]{:S(2)}) collective-permute-start(bf16[1,128,128]{1,2,0:T(8,128)(2,1)S(1)} %fusion.361), channel_id=1, source_target_pairs={{0,64},{64,128},{128,192},{192,256},{256,320},{320,384},{384,448},... | collective-permute-start | bytes 98312 | tf_op jit(solution)/shard_map/while/body/eval_jaxpr/ppermute | solution.py:29
  958.1 23.7 %collective-permute-start.6 = (bf16[1,128,128]{1,2,0:T(8,128)(2,1)S(1)}, bf16[1,128,128]{1,2,0:T(8,128)(2,1)S(1)}, u32[]{:S(2)}, u32[]{:S(2)}) collective-permute-start(bf16[1,128,128]{1,2,0:T(8,128)(2,1)S(1)} %fusion.361), channel_id=1, source_target_pairs={{64,0},{128,64},{192,128},{256,192},{320,256},{384,320},{448,384},... | collective-permute-start | bytes 98312 | tf_op jit(solution)/shard_map/while/body/eval_jaxpr/ppermute | solution.py:30
  987.5 46.2 %reduce-scatter.6.cloned.1.call-start = ((), (), s32[]{:S(2)}) async-start(), calls=%async_computation.5 | async-start | bytes 163840 | tf_op jit(solution)/shard_map/while
  1035.4 29.2 %collective-permute-start.7 = (bf16[128,128]{0,1:T(8,128)(2,1)S(1)}, bf16[128,128]{0,1:T(8,128)(2,1)S(1)}, u32[]{:S(2)}, u32[]{:S(2)}) collective-permute-start(bf16[128,128]{0,1:T(8,128)(2,1)S(1)} %convert_select_fusion.2), channel_id=1, source_target_pairs={{0,64},{64,0},{128,192},{192,128},{256,320},{320,256},{384,448},{4... | collective-permute-start | bytes 98312 | tf_op jit(solution)/shard_map/while/body/eval_jaxpr/ppermute | solution.py:19
  1049.1 25.7 %collective-permute-start.5 = (bf16[1,128,128]{1,2,0:T(8,128)(2,1)S(1)}, bf16[1,128,128]{1,2,0:T(8,128)(2,1)S(1)}, u32[]{:S(2)}, u32[]{:S(2)}) collective-permute-start(bf16[1,128,128]{1,2,0:T(8,128)(2,1)S(1)} %fusion.361), channel_id=1, source_target_pairs={{0,64},{64,128},{128,192},{192,256},{256,320},{320,384},{384,448},... | collective-permute-start | bytes 98312 | tf_op jit(solution)/shard_map/while/body/eval_jaxpr/ppermute | solution.py:29
  1051.0 23.7 %collective-permute-start.6 = (bf16[1,128,128]{1,2,0:T(8,128)(2,1)S(1)}, bf16[1,128,128]{1,2,0:T(8,128)(2,1)S(1)}, u32[]{:S(2)}, u32[]{:S(2)}) collective-permute-start(bf16[1,128,128]{1,2,0:T(8,128)(2,1)S(1)} %fusion.361), channel_id=1, source_target_pairs={{64,0},{128,64},{192,128},{256,192},{320,256},{384,320},{448,384},... | collective-permute-start | bytes 98312 | tf_op jit(solution)/shard_map/while/body/eval_jaxpr/ppermute | solution.py:30
  1080.4 46.2 %reduce-scatter.6.cloned.1.call-start = ((), (), s32[]{:S(2)}) async-start(), calls=%async_computation.5 | async-start | bytes 163840 | tf_op jit(solution)/shard_map/while
  1128.3 29.2 %collective-permute-start.7 = (bf16[128,128]{0,1:T(8,128)(2,1)S(1)}, bf16[128,128]{0,1:T(8,128)(2,1)S(1)}, u32[]{:S(2)}, u32[]{:S(2)}) collective-permute-start(bf16[128,128]{0,1:T(8,128)(2,1)S(1)} %convert_select_fusion.2), channel_id=1, source_target_pairs={{0,64},{64,0},{128,192},{192,128},{256,320},{320,256},{384,448},{4... | collective-permute-start | bytes 98312 | tf_op jit(solution)/shard_map/while/body/eval_jaxpr/ppermute | solution.py:19
  1142.0 25.6 %collective-permute-start.5 = (bf16[1,128,128]{1,2,0:T(8,128)(2,1)S(1)}, bf16[1,128,128]{1,2,0:T(8,128)(2,1)S(1)}, u32[]{:S(2)}, u32[]{:S(2)}) collective-permute-start(bf16[1,128,128]{1,2,0:T(8,128)(2,1)S(1)} %fusion.361), channel_id=1, source_target_pairs={{0,64},{64,128},{128,192},{192,256},{256,320},{320,384},{384,448},... | collective-permute-start | bytes 98312 | tf_op jit(solution)/shard_map/while/body/eval_jaxpr/ppermute | solution.py:29
  1143.9 23.7 %collective-permute-start.6 = (bf16[1,128,128]{1,2,0:T(8,128)(2,1)S(1)}, bf16[1,128,128]{1,2,0:T(8,128)(2,1)S(1)}, u32[]{:S(2)}, u32[]{:S(2)}) collective-permute-start(bf16[1,128,128]{1,2,0:T(8,128)(2,1)S(1)} %fusion.361), channel_id=1, source_target_pairs={{64,0},{128,64},{192,128},{256,192},{320,256},{384,320},{448,384},... | collective-permute-start | bytes 98312 | tf_op jit(solution)/shard_map/while/body/eval_jaxpr/ppermute | solution.py:30
  1173.3 45.9 %reduce-scatter.6.cloned.1.call-start = ((), (), s32[]{:S(2)}) async-start(), calls=%async_computation.5 | async-start | bytes 163840 | tf_op jit(solution)/shard_map/while
  1221.0 29.2 %collective-permute-start.7 = (bf16[128,128]{0,1:T(8,128)(2,1)S(1)}, bf16[128,128]{0,1:T(8,128)(2,1)S(1)}, u32[]{:S(2)}, u32[]{:S(2)}) collective-permute-start(bf16[128,128]{0,1:T(8,128)(2,1)S(1)} %convert_select_fusion.2), channel_id=1, source_target_pairs={{0,64},{64,0},{128,192},{192,128},{256,320},{320,256},{384,448},{4... | collective-permute-start | bytes 98312 | tf_op jit(solution)/shard_map/while/body/eval_jaxpr/ppermute | solution.py:19
  1234.7 25.6 %collective-permute-start.5 = (bf16[1,128,128]{1,2,0:T(8,128)(2,1)S(1)}, bf16[1,128,128]{1,2,0:T(8,128)(2,1)S(1)}, u32[]{:S(2)}, u32[]{:S(2)}) collective-permute-start(bf16[1,128,128]{1,2,0:T(8,128)(2,1)S(1)} %fusion.361), channel_id=1, source_target_pairs={{0,64},{64,128},{128,192},{192,256},{256,320},{320,384},{384,448},... | collective-permute-start | bytes 98312 | tf_op jit(solution)/shard_map/while/body/eval_jaxpr/ppermute | solution.py:29
  1236.6 23.7 %collective-permute-start.6 = (bf16[1,128,128]{1,2,0:T(8,128)(2,1)S(1)}, bf16[1,128,128]{1,2,0:T(8,128)(2,1)S(1)}, u32[]{:S(2)}, u32[]{:S(2)}) collective-permute-start(bf16[1,128,128]{1,2,0:T(8,128)(2,1)S(1)} %fusion.361), channel_id=1, source_target_pairs={{64,0},{128,64},{192,128},{256,192},{320,256},{384,320},{448,384},... | collective-permute-start | bytes 98312 | tf_op jit(solution)/shard_map/while/body/eval_jaxpr/ppermute | solution.py:30
  1266.0 46.3 %reduce-scatter.6.cloned.1.call-start = ((), (), s32[]{:S(2)}) async-start(), calls=%async_computation.5 | async-start | bytes 163840 | tf_op jit(solution)/shard_map/while
  1314.0 29.2 %collective-permute-start.7 = (bf16[128,128]{0,1:T(8,128)(2,1)S(1)}, bf16[128,128]{0,1:T(8,128)(2,1)S(1)}, u32[]{:S(2)}, u32[]{:S(2)}) collective-permute-start(bf16[128,128]{0,1:T(8,128)(2,1)S(1)} %convert_select_fusion.2), channel_id=1, source_target_pairs={{0,64},{64,0},{128,192},{192,128},{256,320},{320,256},{384,448},{4... | collective-permute-start | bytes 98312 | tf_op jit(solution)/shard_map/while/body/eval_jaxpr/ppermute | solution.py:19
  1327.7 25.6 %collective-permute-start.5 = (bf16[1,128,128]{1,2,0:T(8,128)(2,1)S(1)}, bf16[1,128,128]{1,2,0:T(8,128)(2,1)S(1)}, u32[]{:S(2)}, u32[]{:S(2)}) collective-permute-start(bf16[1,128,128]{1,2,0:T(8,128)(2,1)S(1)} %fusion.361), channel_id=1, source_target_pairs={{0,64},{64,128},{128,192},{192,256},{256,320},{320,384},{384,448},... | collective-permute-start | bytes 98312 | tf_op jit(solution)/shard_map/while/body/eval_jaxpr/ppermute | solution.py:29
  1329.6 23.7 %collective-permute-start.6 = (bf16[1,128,128]{1,2,0:T(8,128)(2,1)S(1)}, bf16[1,128,128]{1,2,0:T(8,128)(2,1)S(1)}, u32[]{:S(2)}, u32[]{:S(2)}) collective-permute-start(bf16[1,128,128]{1,2,0:T(8,128)(2,1)S(1)} %fusion.361), channel_id=1, source_target_pairs={{64,0},{128,64},{192,128},{256,192},{320,256},{384,320},{448,384},... | collective-permute-start | bytes 98312 | tf_op jit(solution)/shard_map/while/body/eval_jaxpr/ppermute | solution.py:30
  1359.0 44.6 %reduce-scatter.6.cloned.1.call-start = ((), (), s32[]{:S(2)}) async-start(), calls=%async_computation.5 | async-start | bytes 163840 | tf_op jit(solution)/shard_map/while
  1405.3 29.1 %collective-permute-start.7 = (bf16[128,128]{0,1:T(8,128)(2,1)S(1)}, bf16[128,128]{0,1:T(8,128)(2,1)S(1)}, u32[]{:S(2)}, u32[]{:S(2)}) collective-permute-start(bf16[128,128]{0,1:T(8,128)(2,1)S(1)} %convert_select_fusion.2), channel_id=1, source_target_pairs={{0,64},{64,0},{128,192},{192,128},{256,320},{320,256},{384,448},{4... | collective-permute-start | bytes 98312 | tf_op jit(solution)/shard_map/while/body/eval_jaxpr/ppermute | solution.py:19
  1419.0 25.7 %collective-permute-start.5 = (bf16[1,128,128]{1,2,0:T(8,128)(2,1)S(1)}, bf16[1,128,128]{1,2,0:T(8,128)(2,1)S(1)}, u32[]{:S(2)}, u32[]{:S(2)}) collective-permute-start(bf16[1,128,128]{1,2,0:T(8,128)(2,1)S(1)} %fusion.361), channel_id=1, source_target_pairs={{0,64},{64,128},{128,192},{192,256},{256,320},{320,384},{384,448},... | collective-permute-start | bytes 98312 | tf_op jit(solution)/shard_map/while/body/eval_jaxpr/ppermute | solution.py:29
  1420.9 23.7 %collective-permute-start.6 = (bf16[1,128,128]{1,2,0:T(8,128)(2,1)S(1)}, bf16[1,128,128]{1,2,0:T(8,128)(2,1)S(1)}, u32[]{:S(2)}, u32[]{:S(2)}) collective-permute-start(bf16[1,128,128]{1,2,0:T(8,128)(2,1)S(1)} %fusion.361), channel_id=1, source_target_pairs={{64,0},{128,64},{192,128},{256,192},{320,256},{384,320},{448,384},... | collective-permute-start | bytes 98312 | tf_op jit(solution)/shard_map/while/body/eval_jaxpr/ppermute | solution.py:30
  1450.3 87.0 %all-gather.5.cloned.1.call-start = ((), (), s32[]{:S(2)}) async-start(), calls=%async_computation.4 | async-start | bytes 4456448 | tf_op jit(solution)/shard_map/all_gather | solution.py:326
  1452.7 14.6 all-to-all-start.1
  1543.3 26.9 %collective-permute-start.13 = (bf16[8,27,512]{2,1,0:T(8,128)(2,1)S(1)}, bf16[8,27,512]{2,1,0:T(8,128)(2,1)S(1)}, u32[]{:S(2)}, u32[]{:S(2)}) collective-permute-start(bf16[8,27,512]{2,1,0:T(8,128)(2,1)S(1)} %pad_maximum_fusion.3), channel_id=1, source_target_pairs={{0,64},{64,0},{128,192},{192,128},{256,320},{320,256},{384,448},{4... | collective-permute-start | bytes 663560 | tf_op jit(solution)/shard_map/ppermute | solution.py:19
  (95 other events, 1766.0 us)
Sparse Core Ops, SparseCore 0:
  62.8 128.8 all-gather.2
  712.9 42.1 reduce-scatter.5
  812.2 35.7 reduce-scatter.5
  922.5 18.2 reduce-scatter.5
  997.9 35.7 reduce-scatter.5
  1090.8 35.7 reduce-scatter.5
  1201.1 18.1 reduce-scatter.5
  1276.4 35.8 reduce-scatter.5
  1369.4 34.1 reduce-scatter.5
  1452.8 84.4 all-gather.4
